TPU v7x, 1024 devices: a whole 8x8x8 slice. The times are simulated.
1024 devices in a mesh: pipe: 16 (over z_hi, x), expert: 64 (over y, z_lo, core).
Axes of the slice: x: 8, y: 8, z: 8 (z_hi: 2, z_lo: 4; z = z_hi * 4 + z_lo), core: 2. Of those that a mesh axis runs over, the one named last changes fastest.
Arguments:
- out_grad: bfloat16 [16, 1, 8192, 1024], P('pipe', None, 'expert'), may hold values from -6 to 6
- gate_weights: float32 [16, 1, 8192, 8], P('pipe', None, 'expert'), may hold values from 0.05 to 1
- routes: int32 [16, 1, 8192, 8], P('pipe', None, 'expert'), may hold values from 0 to 63, as said below
- hidden_act: bfloat16 [16, 1, 64, 1024, 512], P('pipe', None, 'expert'), may hold values from -0.59765625 to 0.59765625
- down_weight: bfloat16 [16, 64, 256, 1024], P('pipe', 'expert'), may hold values from -0.1875 to 0.1875
- block_scales: float32 [16, 64, 2, 8], P('pipe', 'expert'), may hold values from 0.25 to 4
Outputs:
- hidden_grad: bfloat16 [16, 1, 64, 1024, 512], P('pipe', None, 'expert')
- weight_grad: bfloat16 [16, 64, 256, 1024], P('pipe', 'expert')
Inputs may be any that keep to these rules, and one draw needn't show every extreme that they name: `routes`: each token names 8 different experts. Within one section and one micro-batch, the 128 tokens of each aligned block name every expert exactly 16 times.
All inputs are finite; a program needn't handle non-finite values.
Results may differ from a plain program's by a relative error of at most 0.0075.
Values may be sent and summed in bfloat16 or wider, within the bound.
No kernel may reach another device: no remote copies, remote signals or barrier semaphores. Data moves between devices by JAX's collectives and lax.ppermute only.
A program may use at most 32 MiB of HBM per device.

v0:
```python
import jax
import jax.numpy as jnp
from jax import lax
from jax.sharding import PartitionSpec as P

D = 1024
QBLOCK = 128


def partner(block, axis, distance):
    count = lax.axis_size(axis)
    route = []
    for low in range(count):
        high = low | 1 << distance
        if high != low and high < count:
            route += [(low, high), (high, low)]
    return lax.ppermute(block, axis, route)


def expand(scales):
    return jnp.repeat(jnp.repeat(scales, QBLOCK, axis=0), QBLOCK, axis=1)


def on_device(out_grad, gate_weights, routes, hidden_act, down_weight, block_scales):
    experts = lax.axis_size("expert")
    gradient = out_grad[0]
    gate_rows = gate_weights[0]
    route_rows = routes[0]
    tok_count = gradient.shape[1]
    top_count = route_rows.shape[2]
    capacity = tok_count * top_count // experts
    dequant_half = (down_weight[0, 0].astype(jnp.float32) * expand(block_scales[0, 0])).astype(
        jnp.bfloat16
    )
    activations = hidden_act[0, :, 0]
    scaled = (gate_rows[0][:, :, None] * gradient[0][:, None, :].astype(jnp.float32)).astype(
        jnp.bfloat16
    )
    scaled = scaled.reshape(tok_count * top_count, D)
    expert_ids = route_rows[0].reshape(-1)
    onehot = (expert_ids[:, None] == jnp.arange(experts, dtype=jnp.int32)[None, :]).astype(
        jnp.int32
    )
    before = jnp.cumsum(onehot, axis=0) - onehot
    slot_rank = jnp.sum(before * onehot, axis=1)
    slot_index = expert_ids * capacity + slot_rank
    filled = jnp.zeros((experts * capacity, D), jnp.bfloat16).at[slot_index].set(scaled)
    received = [
        lax.all_to_all(
            filled.reshape(experts, capacity, D), "expert", split_axis=0, concat_axis=0, tiled=True
        ).reshape(-1, D)
    ]
    rows_stack = jnp.stack(received)
    sections = lax.axis_size("pipe")
    half_size = sections // 2
    pair_bit = sections.bit_length() - 2
    upper_half = (lax.axis_index("pipe") >= half_size).astype(jnp.int32)
    is_upper = upper_half == 1
    half_rows = dequant_half.shape[0]
    both_dims = (((0, 1), (0, 1)), ((), ()))
    row_dims = (((2,), (1,)), ((), ()))
    other_half = partner(dequant_half, "pipe", pair_bit)
    whole = jnp.where(
        is_upper,
        jnp.concatenate([other_half, dequant_half], axis=0),
        jnp.concatenate([dequant_half, other_half], axis=0),
    )
    hidden = lax.dot_general(
        rows_stack, whole, row_dims, preferred_element_type=jnp.float32
    ).astype(jnp.bfloat16)
    section_sum = lax.dot_general(
        activations, rows_stack, both_dims, preferred_element_type=jnp.float32
    )
    their_part = lax.dynamic_slice_in_dim(
        section_sum, (1 - upper_half) * half_rows, half_rows, 0
    ).astype(jnp.bfloat16)
    received_part = partner(their_part, "pipe", pair_bit)
    own_part = lax.dynamic_slice_in_dim(section_sum, upper_half * half_rows, half_rows, 0)
    rounded = lax.optimization_barrier(own_part.astype(jnp.bfloat16)).astype(jnp.float32)
    weight_grad = (rounded + received_part.astype(jnp.float32)).astype(jnp.bfloat16)
    hidden_grad = hidden[None, :, None]
    return (hidden_grad, weight_grad[None, None])


def solution(mesh):
    in_specs = (
        P("pipe", None, "expert", None),
        P("pipe", None, "expert", None),
        P("pipe", None, "expert", None),
        P("pipe", None, "expert", None, None),
        P("pipe", "expert", None, None),
        P("pipe", "expert", None, None),
    )
    out_specs = (P("pipe", None, "expert", None, None), P("pipe", "expert", None, None))
    return jax.shard_map(
        on_device, mesh=mesh, in_specs=in_specs, out_specs=out_specs, check_vma=False
    )
```

profile of v0, /device:TPU:144, one launch (start us, length us, event | category | flops | bytes accessed | tf_op | source)
XLA Modules:
  0.0 168.9 jit_solution(17413418093403787469)
XLA Ops:
  0.6 0.0 copy-start
  0.6 0.0 copy-start.2
  0.7 0.0 copy-start.3
  0.7 0.8 broadcast_multiply_fusion
  1.5 0.8 copy.10
  2.2 0.1 eq.32
  2.3 0.1 eq.28
  2.4 0.1 copy.9
  2.5 0.1 mul.48
  2.7 18.0 %reduce-window.6 = s32[64,8,128]{2,1,0:T(8,128)S(1)} reduce-window(s32[64,8,128]{2,1,0:T(8,128)S(1)} %fusion.22, s32[]{:T(128)} %constant.7.clone.1), window={size=1x1x128 pad=0_0x0_0x127_0}, to_apply=%region_0.0 | reduce-window | flops 8323072 | bytes 524292 | tf_op jit(solution)/shard_map/reduce-window
  20.7 0.1 slice.8
  20.8 0.1 copy.12
  21.0 0.1 copy.13
  21.1 0.1 broadcast_add_fusion
  21.2 0.0 copy-done.2
  21.3 0.0 copy-done.3
  21.3 0.1 copy.14
  21.4 0.1 mul.50
  21.5 0.1 fusion.21
  21.6 7.2 %scatter_custom_fusion = bf16[1024,1024]{1,0:T(8,128)(2,1)} fusion(s32[1024]{0:T(1024)S(1)} %bitcast.68, f32[128,1024]{1,0:T(8,128)S(1)} %bitcast_convert_fusion, f32[1024]{0:T(1024)S(1)} %mul.50, bf16[]{:T(256)} %constant.10.clone.1), kind=kCustom, calls=%fused_computation.3 | custom fusion | flops 2097152 | bytes 2625538 | tf_op jit(solution)/shard_map/scatter | solution.py:47
  28.8 0.0 copy-start.4
  28.8 15.5 %all-to-all-start = ((bf16[64,16,1024]{2,1,0:T(8,128)(2,1)}), bf16[64,16,1024]{2,1,0:T(8,128)(2,1)S(1)}, u32[]{:S(2)}, u32[]{:S(2)}) async-start(bf16[64,16,1024]{2,1,0:T(8,128)(2,1)} %bitcast.6), calls=%async_computation | async-start | bytes 4194304 | tf_op jit(solution)/shard_map/all_to_all | solution.py:49
  44.3 0.0 copy-done.4
  44.3 0.3 broadcast_in_dim.19
  44.6 2.1 %fusion.6 = bf16[256,1024]{1,0:T(8,128)(2,1)} fusion(f32[32,8,8,128]{3,2,1,0:T(8,128)S(1)} %bitcast.61, bf16[1,1,256,1024]{3,2,1,0:T(8,128)(2,1)} %param.10), kind=kLoop, calls=%fused_computation.9 | loop fusion | flops 786432 | bytes 2097152 | tf_op jit(solution)/shard_map/convert_element_type | solution.py:32
  46.8 11.3 %collective-permute-start = (bf16[256,1024]{1,0:T(8,128)(2,1)}, bf16[256,1024]{1,0:T(8,128)(2,1)}, u32[]{:S(2)}, u32[]{:S(2)}) collective-permute-start(bf16[256,1024]{1,0:T(8,128)(2,1)} %fusion.6), channel_id=1, source_target_pairs={{0,512},{512,0},{64,576},{576,64},{128,640},{640,128},{192,704},{7... | collective-permute-start | bytes 1572872 | tf_op jit(solution)/shard_map/ppermute | solution.py:17
  58.1 54.2 %all-to-all-done = bf16[64,16,1024]{2,1,0:T(8,128)(2,1)S(1)} async-done(((bf16[64,16,1024]{2,1,0:T(8,128)(2,1)}), bf16[64,16,1024]{2,1,0:T(8,128)(2,1)S(1)}, u32[]{:S(2)}, u32[]{:S(2)}) %all-to-all-start) | async-done | bytes 2097184 | tf_op jit(solution)/shard_map/all_to_all | solution.py:49
  112.3 0.0 copy-done
  112.3 1.3 fusion.12
  113.6 1.1 fusion.16
  114.6 33.8 %collective-permute-start.1 = (bf16[256,1024]{0,1:T(8,128)(2,1)}, bf16[256,1024]{0,1:T(8,128)(2,1)}, u32[]{:S(2)}, u32[]{:S(2)}) collective-permute-start(bf16[256,1024]{0,1:T(8,128)(2,1)} %get-tuple-element.7), channel_id=1, source_target_pairs={{0,512},{512,0},{64,576},{576,64},{128,640},{640,128},{192,704},{7... | collective-permute-start | bytes 1572872 | tf_op jit(solution)/shard_map/ppermute | solution.py:17
  148.5 0.0 copy-start.1
  148.5 0.0 collective-permute-done
  148.5 3.8 %fusion.5 = bf16[1,1,1,1024,512]{4,3,2,1,0:T(8,128)(2,1)} fusion(bf16[1024,1024]{1,0:T(8,128)(2,1)S(1)} %bitcast.63, bf16[256,1024]{1,0:T(8,128)(2,1)} %fusion.6, bf16[256,1024]{1,0:T(8,128)(2,1)} %collective-permute-done, pred[]{:T(512)S(6)} %eq.36), kind=kOutput, calls=%fused_computation.7 | convolution fusion | flops 1078984704 | bytes 4194305 | tf_op jit(solution)/shard_map/dot_general | solution.py:68
  152.3 14.4 %collective-permute-done.1 = bf16[256,1024]{0,1:T(8,128)(2,1)} collective-permute-done((bf16[256,1024]{0,1:T(8,128)(2,1)}, bf16[256,1024]{0,1:T(8,128)(2,1)}, u32[]{:S(2)}, u32[]{:S(2)}) %collective-permute-start.1) | collective-permute-done | bytes 524320 | tf_op jit(solution)/shard_map/ppermute | solution.py:17
  166.7 0.0 copy-done.1
  166.7 1.2 fusion.18
  167.9 1.0 copy.15
  (6 shorter events, 0.1 us)
Async XLA Ops:
  0.6 111.7 %copy-start = (bf16[1,1,1,1024,512]{4,3,2,1,0:T(8,128)(2,1)S(1)}, bf16[1,1,1,1024,512]{4,3,2,1,0:T(8,128)(2,1)}, u32[]{:S(2)}) copy-start(bf16[1,1,1,1024,512]{4,3,2,1,0:T(8,128)(2,1)} %param.9) | copy-start | bytes 3145732
  0.6 20.6 %copy-start.2 = (bf16[1,1,128,1024]{3,2,1,0:T(8,128)(2,1)S(1)}, bf16[1,1,128,1024]{3,2,1,0:T(8,128)(2,1)}, u32[]{:S(2)}) copy-start(bf16[1,1,128,1024]{3,2,1,0:T(8,128)(2,1)} %param.6) | copy-start | bytes 786436
  0.7 20.6 %copy-start.3 = (f32[1,1,128,8]{2,3,1,0:T(8,128)S(1)}, f32[1,1,128,8]{2,3,1,0:T(8,128)}, u32[]{:S(2)}) copy-start(f32[1,1,128,8]{2,3,1,0:T(8,128)} %param.7) | copy-start | bytes 12292
  28.8 15.5 %copy-start.4 = (f32[1,1,2,8]{3,2,1,0:T(2,128)S(1)}, f32[1,1,2,8]{3,2,1,0:T(2,128)}, u32[]{:S(2)}) copy-start(f32[1,1,2,8]{3,2,1,0:T(2,128)} %param.11) | copy-start | bytes 196
  28.8 83.5 %all-to-all-start = ((bf16[64,16,1024]{2,1,0:T(8,128)(2,1)}), bf16[64,16,1024]{2,1,0:T(8,128)(2,1)S(1)}, u32[]{:S(2)}, u32[]{:S(2)}) async-start(bf16[64,16,1024]{2,1,0:T(8,128)(2,1)} %bitcast.6), calls=%async_computation | async-start | bytes 4194304 | tf_op jit(solution)/shard_map/all_to_all | solution.py:49
  46.8 101.7 %collective-permute-start = (bf16[256,1024]{1,0:T(8,128)(2,1)}, bf16[256,1024]{1,0:T(8,128)(2,1)}, u32[]{:S(2)}, u32[]{:S(2)}) collective-permute-start(bf16[256,1024]{1,0:T(8,128)(2,1)} %fusion.6), channel_id=1, source_target_pairs={{0,512},{512,0},{64,576},{576,64},{128,640},{640,128},{192,704},{7... | collective-permute-start | bytes 1572872 | tf_op jit(solution)/shard_map/ppermute | solution.py:17
  114.6 52.1 %collective-permute-start.1 = (bf16[256,1024]{0,1:T(8,128)(2,1)}, bf16[256,1024]{0,1:T(8,128)(2,1)}, u32[]{:S(2)}, u32[]{:S(2)}) collective-permute-start(bf16[256,1024]{0,1:T(8,128)(2,1)} %get-tuple-element.7), channel_id=1, source_target_pairs={{0,512},{512,0},{64,576},{576,64},{128,640},{640,128},{192,704},{7... | collective-permute-start | bytes 1572872 | tf_op jit(solution)/shard_map/ppermute | solution.py:17
  148.5 18.3 %copy-start.1 = (bf16[256,1024]{0,1:T(8,128)(2,1)S(1)}, bf16[256,1024]{0,1:T(8,128)(2,1)}, u32[]{:S(2)}) copy-start(bf16[256,1024]{0,1:T(8,128)(2,1)} %get-tuple-element.6) | copy-start | bytes 1572868
where the time goes:
time: 169 us
  waiting for transfers between devices  68.6 us (41%)
  starting transfers between devices  60.6 us (36%)
  other arithmetic  29.7 us (18%)
  matrix products  5.11 us (3%)
  local copies, waits for them, and re-layouts  4.15 us (2%)
    all_to_all x1, waiting for transfers between devices, on_device(): lax.all_to_all(filled.reshape(experts, capacity, D), 'expert', split_axis...  54.2 us
    ppermute x2, starting transfers between devices, partner(): return lax.ppermute(block, axis, route)  45.1 us
    another operation x3, other arithmetic  18.2 us
    all_to_all x1, starting transfers between devices, on_device(): lax.all_to_all(filled.reshape(experts, capacity, D), 'expert', split_axis...  15.5 us
    ppermute x2, waiting for transfers between devices, partner(): return lax.ppermute(block, axis, route)  14.4 us
    scatter x1, other arithmetic, on_device(): jnp.zeros((experts * capacity, D), jnp.bfloat16).at[slot_index].set(scaled)  7.24 us
    dot_general x1, matrix products, on_device(): lax.dot_general(rows_stack, whole, row_dims, preferred_element_type=jnp.f...  3.83 us
  transfers between devices with their start and end apart: 3, of which 2 were waited for; matrix products, arithmetic and copies ran while one was open for 5% of the time, Pallas kernels for 0%

commit v1 on v0

v1 whole, which is shorter than its diff:
```python
import functools

import jax
import jax.numpy as jnp
from jax import lax
from jax.experimental import pallas as pl
from jax.experimental.pallas import tpu as pltpu
from jax.sharding import PartitionSpec as P

D = 1024
QBLOCK = 128
CHUNKS = 2
BF = jnp.bfloat16
F32 = jnp.float32
VM = pl.BlockSpec(memory_space=pltpu.VMEM)
SM = pl.BlockSpec(memory_space=pltpu.SMEM)


def cost(flops, nbytes):
    return pl.CostEstimate(flops=flops, bytes_accessed=nbytes, transcendentals=0)


def dequant_kernel(scale_ref, weight_ref, out_ref):
    rows, cols = weight_ref.shape
    for i in range(rows // QBLOCK):
        for j in range(cols // QBLOCK):
            at = (pl.ds(i * QBLOCK, QBLOCK), pl.ds(j * QBLOCK, QBLOCK))
            out_ref[at] = (weight_ref[at].astype(F32) * scale_ref[i, j]).astype(BF)


def dequantize(weight, scales):
    return pl.pallas_call(
        dequant_kernel,
        out_shape=jax.ShapeDtypeStruct(weight.shape, BF),
        in_specs=[SM, VM],
        out_specs=VM,
        name="dequant",
        cost_estimate=cost(weight.size, weight.size * 4),
    )(scales, weight)


def dispatch_kernel(route_ref, gate_ref, grad_ref, *out_refs):
    top, toks = route_ref.shape
    experts, cap, width = out_refs[0].shape
    routes, gates = route_ref[...], gate_ref[...]
    ids = lax.broadcasted_iota(jnp.int32, (experts, toks), 0)
    member = jnp.zeros((experts, toks), F32)
    gate = jnp.zeros((experts, toks), F32)
    for k in range(top):
        hit = routes[k : k + 1, :] == ids
        member = jnp.where(hit, 1.0, member)
        gate = jnp.where(hit, gates[k : k + 1, :], gate)
    earlier = lax.broadcasted_iota(jnp.int32, (toks, toks), 0)
    later = lax.broadcasted_iota(jnp.int32, (toks, toks), 1)
    upper = jnp.where(earlier < later, 1.0, 0.0).astype(BF)
    rank = jnp.dot(member.astype(BF), upper, preferred_element_type=F32)
    rank = jnp.where(member > 0.0, rank, -1.0)
    places = lax.broadcasted_iota(jnp.int32, (experts, cap, toks), 1).astype(F32)
    pick = rank[:, None, :] == places
    weight = jnp.sum(jnp.where(pick, gate[:, None, :], 0.0), axis=2, keepdims=True)
    weight = weight.reshape(experts * cap, 1)
    pick = jnp.where(pick, 1.0, 0.0).reshape(experts * cap, toks).astype(BF)
    for c, out_ref in enumerate(out_refs):
        rows = jnp.dot(
            pick, grad_ref[:, c * width : (c + 1) * width], preferred_element_type=F32
        )
        out_ref[...] = (rows * weight).astype(BF).reshape(experts, cap, width)


def dispatch(routes, gates, grad, experts, cap):
    toks, d = grad.shape
    width = d // CHUNKS
    return pl.pallas_call(
        dispatch_kernel,
        out_shape=[jax.ShapeDtypeStruct((experts, cap, width), BF)] * CHUNKS,
        in_specs=[VM, VM, VM],
        out_specs=[VM] * CHUNKS,
        name="dispatch",
        cost_estimate=cost(2 * experts * cap * toks * d, experts * cap * d * 2),
    )(routes, gates, grad)


ROWS_ROWS = (((0,), (0,)), ((), ()))
COLS_COLS = (((1,), (1,)), ((), ()))


def theirs_kernel(half_ref, act_ref, rows_ref, out_ref):
    out_ref[...] = lax.dot_general(
        act_ref[...], rows_ref[...], ROWS_ROWS, preferred_element_type=F32
    ).astype(BF)


def part_grad(half, act, rows, name):
    slots, ff = act.shape
    width = rows.shape[1]
    return pl.pallas_call(
        theirs_kernel,
        grid_spec=pltpu.PrefetchScalarGridSpec(
            num_scalar_prefetch=1,
            grid=(1,),
            in_specs=[
                pl.BlockSpec((slots, ff // 2), lambda i, h: (0, h[0])),
                pl.BlockSpec((slots, width), lambda i, h: (0, 0)),
            ],
            out_specs=pl.BlockSpec((ff // 2, width), lambda i, h: (0, 0)),
        ),
        out_shape=jax.ShapeDtypeStruct((ff // 2, width), BF),
        name=name,
        cost_estimate=cost(ff * width * slots, slots * width * 2 + slots * ff),
    )(half, act, rows)


def hidden_kernel(half_ref, own_ref, other_ref, *refs):
    row_refs, out_ref = refs[:-1], refs[-1]

    def product(weight_ref):
        total = None
        at = 0
        for row_ref in row_refs:
            width = row_ref.shape[1]
            term = lax.dot_general(
                row_ref[...],
                weight_ref[:, at : at + width],
                COLS_COLS,
                preferred_element_type=F32,
            )
            total = term if total is None else total + term
            at += width
        out_ref[...] = total.astype(BF)

    @pl.when(pl.program_id(1) == 0)
    def _():
        product(own_ref)

    @pl.when(pl.program_id(1) == 1)
    def _():
        product(other_ref)


def hidden(half, own, other, rows):
    slots = rows[0].shape[0]
    half_rows, d = own.shape
    block = 256
    return pl.pallas_call(
        hidden_kernel,
        grid_spec=pltpu.PrefetchScalarGridSpec(
            num_scalar_prefetch=1,
            grid=(slots // block, 2),
            in_specs=[pl.BlockSpec((half_rows, d), lambda i, j, h: (0, 0))] * 2
            + [pl.BlockSpec((block, r.shape[1]), lambda i, j, h: (i, 0)) for r in rows],
            out_specs=pl.BlockSpec(
                (block, half_rows), lambda i, j, h: (i, h[0] + j - 2 * h[0] * j)
            ),
        ),
        out_shape=jax.ShapeDtypeStruct((slots, 2 * half_rows), BF),
        name="hidden",
        cost_estimate=cost(4 * slots * half_rows * d, slots * d * 2 + slots * half_rows * 4),
    )(half, own, other, *rows)


def add_kernel(*refs):
    ins, out_ref = refs[:-1], refs[-1]
    at = 0
    for own_ref, got_ref in zip(ins[::2], ins[1::2]):
        width = own_ref.shape[1]
        out_ref[:, at : at + width] = (
            own_ref[...].astype(F32) + got_ref[...].astype(F32)
        ).astype(BF)
        at += width


def add_parts(pairs):
    rows = pairs[0][0].shape[0]
    d = sum(p[0].shape[1] for p in pairs)
    flat = [x for p in pairs for x in p]
    return pl.pallas_call(
        add_kernel,
        out_shape=jax.ShapeDtypeStruct((rows, d), BF),
        in_specs=[VM] * len(flat),
        out_specs=VM,
        name="add_parts",
        cost_estimate=cost(rows * d, rows * d * 6),
    )(*flat)


def partner(block):
    count = lax.axis_size("pipe")
    route = [(i, (i + count // 2) % count) for i in range(count)]
    return lax.ppermute(block, "pipe", route)


def on_device(out_grad, gate_weights, routes, hidden_act, down_weight, block_scales):
    experts = lax.axis_size("expert")
    grad = out_grad[0, 0]
    toks = grad.shape[0]
    cap = toks * routes.shape[3] // experts
    upper = (lax.axis_index("pipe") >= lax.axis_size("pipe") // 2).astype(jnp.int32)
    mine, theirs = upper.reshape(1), (1 - upper).reshape(1)
    act = hidden_act[0, 0, 0]

    blocks = dispatch(routes[0, 0].T, gate_weights[0, 0].T, grad, experts, cap)
    own_half = dequantize(down_weight[0, 0], block_scales[0, 0])
    own_half, *rest = lax.optimization_barrier((own_half, *blocks[1:]))
    blocks = [blocks[0], *rest]
    got = [
        lax.all_to_all(b, "expert", 0, 0, tiled=True).reshape(experts * cap, -1)
        for b in blocks
    ]
    other_half = partner(own_half)
    sent = [partner(part_grad(theirs, act, r, "theirs")) for r in got]
    kept = [part_grad(mine, act, r, "kept") for r in got]
    hidden_grad = hidden(mine, own_half, other_half, got)
    weight_grad = add_parts(list(zip(kept, sent)))
    return hidden_grad[None, None, None], weight_grad[None, None]


def solution(mesh):
    row = P("pipe", None, "expert", None)
    in_specs = (
        row,
        row,
        row,
        P("pipe", None, "expert", None, None),
        P("pipe", "expert", None, None),
        P("pipe", "expert", None, None),
    )
    out_specs = (P("pipe", None, "expert", None, None), P("pipe", "expert", None, None))
    return jax.shard_map(
        on_device, mesh=mesh, in_specs=in_specs, out_specs=out_specs, check_vma=False
    )
```

time: 169 us -> 148 us (0.88)
  the two profiles are of different devices: /device:TPU:144 before, /device:TPU:140 now
where the time goes in v1:
time: 148 us; the launch traced here: 147 us
  waiting for transfers between devices  74.1 us (50%)
  starting transfers between devices  44.9 us (30%)
  Pallas kernels  24.4 us (16%)
  local copies, waits for them, and re-layouts  3.21 us (2%)
    all_to_all x2, waiting for transfers between devices, on_device(): lax.all_to_all(b, 'expert', 0, 0, tiled=True).reshape(experts * cap, -1)  74.1 us
    ppermute x3, starting transfers between devices, partner(): return lax.ppermute(block, 'pipe', route)  24.2 us
    all_to_all x2, starting transfers between devices, on_device(): lax.all_to_all(b, 'expert', 0, 0, tiled=True).reshape(experts * cap, -1)  20.8 us
    pallas_call x4, Pallas kernels, part_grad(): pl.pallas_call(theirs_kernel, grid_spec=pltpu.PrefetchScalarGridSpec(num_...  10.3 us
    pallas_call x1, Pallas kernels, hidden(): pl.pallas_call(hidden_kernel, grid_spec=pltpu.PrefetchScalarGridSpec(num_...  7.12 us
    unnamed x12, local copies, waits for them, and re-layouts  3.21 us
  transfers between devices with their start and end apart: 5, of which 2 were waited for; matrix products, arithmetic and copies ran while one was open for 0% of the time, Pallas kernels for 13%

profile of v1, /device:TPU:140, one launch (start us, length us, event | category | flops | bytes accessed | tf_op | source)
XLA Modules:
  0.0 147.4 jit_solution(5709595845772165092)
XLA Ops:
  0.6 2.9 %dispatch.1 = (bf16[64,16,512]{2,1,0:T(8,128)(2,1)}, bf16[64,16,512]{2,1,0:T(8,128)(2,1)}) custom-call(s32[8,128]{1,0:T(8,128)} %bitcast.31, f32[8,128]{1,0:T(8,128)} %bitcast.32, bf16[128,1024]{1,0:T(8,128)(2,1)} %bitcast.30), custom_call_target="tpu_custom_call" | custom-call | flops 268435456 | bytes 2097152 | tf_op jit(solution)/shard_map/dispatch/pallas_call | solution.py:73
  3.5 15.0 %all-to-all-start = ((bf16[64,16,512]{2,1,0:T(8,128)(2,1)}), bf16[64,16,512]{2,1,0:T(8,128)(2,1)S(1)}, u32[]{:S(2)}, u32[]{:S(2)}) async-start(bf16[64,16,512]{2,1,0:T(8,128)(2,1)} %get-tuple-element.8), calls=%async_computation | async-start | bytes 2097152 | tf_op jit(solution)/shard_map/all_to_all | solution.py:206
  18.6 2.0 %dequant.1.own_ref = bf16[256,1024]{1,0:T(8,128)(2,1)} custom-call(f32[2,8]{1,0:T(2,128)} %bitcast.29, bf16[256,1024]{1,0:T(8,128)(2,1)} %bitcast.28), custom_call_target="tpu_custom_call" | custom-call | flops 262144 | bytes 1048576 | tf_op jit(solution)/shard_map/dequant/pallas_call | solution.py:32
  20.6 0.0 copy-start.2
  20.6 26.8 %all-to-all-done = bf16[64,16,512]{2,1,0:T(8,128)(2,1)S(1)} async-done(((bf16[64,16,512]{2,1,0:T(8,128)(2,1)}), bf16[64,16,512]{2,1,0:T(8,128)(2,1)S(1)}, u32[]{:S(2)}, u32[]{:S(2)}) %all-to-all-start) | async-done | bytes 1048608 | tf_op jit(solution)/shard_map/all_to_all | solution.py:206
  47.3 0.0 copy-start
  47.3 5.7 %all-to-all-start.1 = ((bf16[64,16,512]{2,1,0:T(8,128)(2,1)}), bf16[64,16,512]{2,1,0:T(8,128)(2,1)S(1)}, u32[]{:S(2)}, u32[]{:S(2)}) async-start(bf16[64,16,512]{2,1,0:T(8,128)(2,1)} %get-tuple-element.9), calls=%async_computation.1 | async-start | bytes 2097152 | tf_op jit(solution)/shard_map/all_to_all | solution.py:206
  53.1 0.0 copy-done.2
  53.1 11.9 %collective-permute-start = (bf16[256,1024]{1,0:T(8,128)(2,1)S(1)}, bf16[256,1024]{1,0:T(8,128)(2,1)S(1)}, u32[]{:S(2)}, u32[]{:S(2)}) collective-permute-start(bf16[256,1024]{1,0:T(8,128)(2,1)S(1)} %copy-done.2), channel_id=1, source_target_pairs={{0,512},{64,576},{128,640},{192,704},{256,768},{320,832},{384,896}... | collective-permute-start | bytes 1572872 | tf_op jit(solution)/shard_map/ppermute | solution.py:189
  65.0 0.0 copy-done
  65.0 2.6 %theirs.2 = bf16[256,512]{1,0:T(8,128)(2,1)} custom-call(s32[1]{0:T(128)} %bitcast.12.half_ref, bf16[1024,512]{1,0:T(8,128)(2,1)} %bitcast.16, bf16[1024,512]{1,0:T(8,128)(2,1)} %bitcast.20), custom_call_target="tpu_custom_call" | custom-call | flops 268435456 | bytes 1572864 | tf_op jit(solution)/shard_map/theirs/pallas_call | solution.py:96
  67.6 1.9 %collective-permute-start.1 = (bf16[256,512]{1,0:T(8,128)(2,1)}, bf16[256,512]{1,0:T(8,128)(2,1)S(1)}, u32[]{:S(2)}, u32[]{:S(2)}) collective-permute-start(bf16[256,512]{1,0:T(8,128)(2,1)} %theirs.2), channel_id=1, source_target_pairs={{0,512},{64,576},{128,640},{192,704},{256,768},{320,832},{384,896}... | collective-permute-start | bytes 786440 | tf_op jit(solution)/shard_map/ppermute | solution.py:189
  69.5 47.3 %all-to-all-done.1 = bf16[64,16,512]{2,1,0:T(8,128)(2,1)S(1)} async-done(((bf16[64,16,512]{2,1,0:T(8,128)(2,1)}), bf16[64,16,512]{2,1,0:T(8,128)(2,1)S(1)}, u32[]{:S(2)}, u32[]{:S(2)}) %all-to-all-start.1) | async-done | bytes 1048608 | tf_op jit(solution)/shard_map/all_to_all | solution.py:206
  116.8 0.0 copy-start.1
  116.8 1.0 copy-done.1
  117.8 2.6 %theirs.3 = bf16[256,512]{1,0:T(8,128)(2,1)} custom-call(s32[1]{0:T(128)} %bitcast.12.half_ref, bf16[1024,512]{1,0:T(8,128)(2,1)} %bitcast.17, bf16[1024,512]{1,0:T(8,128)(2,1)} %bitcast.23), custom_call_target="tpu_custom_call" | custom-call | flops 268435456 | bytes 1572864 | tf_op jit(solution)/shard_map/theirs/pallas_call | solution.py:96
  120.4 10.4 %collective-permute-start.2 = (bf16[256,512]{1,0:T(8,128)(2,1)}, bf16[256,512]{1,0:T(8,128)(2,1)S(1)}, u32[]{:S(2)}, u32[]{:S(2)}) collective-permute-start(bf16[256,512]{1,0:T(8,128)(2,1)} %theirs.3), channel_id=1, source_target_pairs={{0,512},{64,576},{128,640},{192,704},{256,768},{320,832},{384,896}... | collective-permute-start | bytes 786440 | tf_op jit(solution)/shard_map/ppermute | solution.py:189
  130.8 2.6 %kept.2.refs_0_ = bf16[256,512]{1,0:T(8,128)(2,1)} custom-call(s32[1]{0:T(128)} %bitcast.half_ref, bf16[1024,512]{1,0:T(8,128)(2,1)} %bitcast.18, bf16[1024,512]{1,0:T(8,128)(2,1)} %bitcast.21), custom_call_target="tpu_custom_call" | custom-call | flops 268435456 | bytes 1572864 | tf_op jit(solution)/shard_map/kept/pallas_call | solution.py:96
  133.4 2.6 %kept.3.refs_2_ = bf16[256,512]{1,0:T(8,128)(2,1)} custom-call(s32[1]{0:T(128)} %bitcast.half_ref, bf16[1024,512]{1,0:T(8,128)(2,1)} %bitcast.19, bf16[1024,512]{1,0:T(8,128)(2,1)} %bitcast.24), custom_call_target="tpu_custom_call" | custom-call | flops 268435456 | bytes 1572864 | tf_op jit(solution)/shard_map/kept/pallas_call | solution.py:96
  135.9 0.0 collective-permute-done.other_ref
  135.9 0.0 copy-start.3
  135.9 0.8 copy-done.3
  136.7 7.1 %hidden.1 = bf16[1024,512]{1,0:T(8,128)(2,1)} custom-call(s32[1]{0:T(128)} %bitcast.half_ref, bf16[256,1024]{1,0:T(8,128)(2,1)} %dequant.1.own_ref, bf16[256,1024]{1,0:T(8,128)(2,1)} %copy-done.3, bf16[1024,512]{1,0:T(8,128)(2,1)} %bitcast.22, bf16[1024,512]{1,0:T(8,128)(2,1)} %bitcast.25), custom_call_target="tpu_custom_call" | custom-call | flops 1073741824 | bytes 3145728 | tf_op jit(solution)/shard_map/hidden/pallas_call | solution.py:144
  143.8 0.0 collective-permute-done.1.refs_1_
  143.8 0.0 copy-start.4
  143.8 0.0 collective-permute-done.2.refs_3_
  143.8 0.7 copy-done.4
  144.6 0.0 copy-start.5
  144.6 0.7 copy-done.5
  145.3 2.1 %add_parts.1 = bf16[256,1024]{1,0:T(8,128)(2,1)} custom-call(bf16[256,512]{1,0:T(8,128)(2,1)} %kept.2.refs_0_, bf16[256,512]{1,0:T(8,128)(2,1)} %copy-done.4, bf16[256,512]{1,0:T(8,128)(2,1)} %kept.3.refs_2_, bf16[256,512]{1,0:T(8,128)(2,1)} %copy-done.5), custom_call_target="tpu_custom_call" | custom-call | flops 262144 | bytes 1572864 | tf_op jit(solution)/shard_map/add_parts/pallas_call | solution.py:176
Async XLA Ops:
  3.5 43.8 %all-to-all-start = ((bf16[64,16,512]{2,1,0:T(8,128)(2,1)}), bf16[64,16,512]{2,1,0:T(8,128)(2,1)S(1)}, u32[]{:S(2)}, u32[]{:S(2)}) async-start(bf16[64,16,512]{2,1,0:T(8,128)(2,1)} %get-tuple-element.8), calls=%async_computation | async-start | bytes 2097152 | tf_op jit(solution)/shard_map/all_to_all | solution.py:206
  20.6 32.5 %copy-start.2 = (bf16[256,1024]{1,0:T(8,128)(2,1)S(1)}, bf16[256,1024]{1,0:T(8,128)(2,1)}, u32[]{:S(2)}) copy-start(bf16[256,1024]{1,0:T(8,128)(2,1)} %dequant.1.own_ref) | copy-start | bytes 1572868
  47.3 17.6 %copy-start = (bf16[64,16,512]{2,1,0:T(8,128)(2,1)}, bf16[64,16,512]{2,1,0:T(8,128)(2,1)S(1)}, u32[]{:S(2)}) copy-start(bf16[64,16,512]{2,1,0:T(8,128)(2,1)S(1)} %all-to-all-done) | copy-start | bytes 3145732
  47.3 69.5 %all-to-all-start.1 = ((bf16[64,16,512]{2,1,0:T(8,128)(2,1)}), bf16[64,16,512]{2,1,0:T(8,128)(2,1)S(1)}, u32[]{:S(2)}, u32[]{:S(2)}) async-start(bf16[64,16,512]{2,1,0:T(8,128)(2,1)} %get-tuple-element.9), calls=%async_computation.1 | async-start | bytes 2097152 | tf_op jit(solution)/shard_map/all_to_all | solution.py:206
  53.1 82.8 %collective-permute-start = (bf16[256,1024]{1,0:T(8,128)(2,1)S(1)}, bf16[256,1024]{1,0:T(8,128)(2,1)S(1)}, u32[]{:S(2)}, u32[]{:S(2)}) collective-permute-start(bf16[256,1024]{1,0:T(8,128)(2,1)S(1)} %copy-done.2), channel_id=1, source_target_pairs={{0,512},{64,576},{128,640},{192,704},{256,768},{320,832},{384,896}... | collective-permute-start | bytes 1572872 | tf_op jit(solution)/shard_map/ppermute | solution.py:189
  67.6 76.3 %collective-permute-start.1 = (bf16[256,512]{1,0:T(8,128)(2,1)}, bf16[256,512]{1,0:T(8,128)(2,1)S(1)}, u32[]{:S(2)}, u32[]{:S(2)}) collective-permute-start(bf16[256,512]{1,0:T(8,128)(2,1)} %theirs.2), channel_id=1, source_target_pairs={{0,512},{64,576},{128,640},{192,704},{256,768},{320,832},{384,896}... | collective-permute-start | bytes 786440 | tf_op jit(solution)/shard_map/ppermute | solution.py:189
  116.8 1.0 copy-start.1
  120.4 23.5 %collective-permute-start.2 = (bf16[256,512]{1,0:T(8,128)(2,1)}, bf16[256,512]{1,0:T(8,128)(2,1)S(1)}, u32[]{:S(2)}, u32[]{:S(2)}) collective-permute-start(bf16[256,512]{1,0:T(8,128)(2,1)} %theirs.3), channel_id=1, source_target_pairs={{0,512},{64,576},{128,640},{192,704},{256,768},{320,832},{384,896}... | collective-permute-start | bytes 786440 | tf_op jit(solution)/shard_map/ppermute | solution.py:189
  135.9 0.8 copy-start.3
  143.8 0.7 copy-start.4
  144.6 0.7 copy-start.5

commit v2 on v1

v2 whole, which is shorter than its diff:
```python
import jax
import jax.numpy as jnp
from jax import lax
from jax.experimental import pallas as pl
from jax.experimental.pallas import tpu as pltpu
from jax.sharding import PartitionSpec as P

QBLOCK = 128
SHARE = 4
CHUNKS = 2
BF = jnp.bfloat16
F32 = jnp.float32
VM = pl.BlockSpec(memory_space=pltpu.VMEM)
SM = pl.BlockSpec(memory_space=pltpu.SMEM)


def cost(flops, nbytes):
    return pl.CostEstimate(flops=flops, bytes_accessed=nbytes, transcendentals=0)


def dequant_kernel(scale_ref, weight_ref, out_ref):
    rows, cols = weight_ref.shape
    for i in range(rows // QBLOCK):
        for j in range(cols // QBLOCK):
            here, there = pl.ds(i * QBLOCK, QBLOCK), pl.ds(j * QBLOCK, QBLOCK)
            block = weight_ref[here, there].astype(F32) * scale_ref[i, j]
            out_ref[there, here] = block.T.astype(BF)


def dequantize(weight, scales):
    return pl.pallas_call(
        dequant_kernel,
        out_shape=jax.ShapeDtypeStruct(weight.shape[::-1], BF),
        in_specs=[SM, VM],
        out_specs=VM,
        name="dequant",
        cost_estimate=cost(weight.size, weight.size * 4),
    )(scales, weight)


def pack_kernel(route_ref, gate_ref, grad_ref, first_ref, *rest):
    toks = grad_ref.shape[0]
    width = first_ref.shape[1]
    top = route_ref.shape[0]
    gate = gate_ref[...]
    high = gate.astype(BF)
    left = gate - high.astype(F32)
    middle = left.astype(BF)
    low = (left - middle.astype(F32)).astype(BF)
    first_ref[:toks, :] = grad_ref[:, :width]
    first_ref[toks:, :] = jnp.zeros((first_ref.shape[0] - toks, width), BF)
    pairs = ((route_ref[...].astype(F32), high), (middle, low))
    for at, (a, b) in enumerate(pairs):
        both = jnp.concatenate([a.astype(F32), b.astype(F32)], axis=0)
        first_ref[toks : toks + 2 * top, at * toks : (at + 1) * toks] = both.astype(BF)
    for c, ref in enumerate(rest):
        ref[...] = grad_ref[:, (c + 1) * width : (c + 2) * width]


def pack(routes, gates, grad):
    toks, d = grad.shape
    top = routes.shape[0]
    width = d // CHUNKS
    shapes = [(toks + 2 * top, width)] + [(toks, width)] * (CHUNKS - 1)
    return pl.pallas_call(
        pack_kernel,
        out_shape=[jax.ShapeDtypeStruct(s, BF) for s in shapes],
        in_specs=[VM, VM, VM],
        out_specs=[VM] * CHUNKS,
        name="pack",
        cost_estimate=cost(grad.size, grad.size * 4),
    )(routes, gates, grad)


def dispatch_kernel(toks, where_ref, own_meta, got_meta, own_ref, got_ref, out_ref):
    members, _, cap, width = out_ref.shape
    side = where_ref[0]
    line = lax.broadcasted_iota(jnp.int32, (members, toks), 0)
    ids = (line // SHARE) * (2 * SHARE) + side * SHARE + line % SHARE
    earlier = lax.broadcasted_iota(jnp.int32, (toks, toks), 0)
    later = lax.broadcasted_iota(jnp.int32, (toks, toks), 1)
    upper = jnp.where(earlier < later, 1.0, 0.0).astype(BF)
    places = lax.broadcasted_iota(jnp.int32, (members, cap, toks), 1).astype(F32)
    for meta_ref, rows_ref, at in ((own_meta, own_ref, side), (got_meta, got_ref, 1 - side)):
        meta = meta_ref[toks:, : 2 * toks].astype(F32)
        top = meta.shape[0] // 2
        routes = meta[:top, :toks].astype(jnp.int32)
        gates = meta[top:, :toks] + (meta[:top, toks:] + meta[top:, toks:])
        member = jnp.zeros((members, toks), F32)
        gate = jnp.zeros((members, toks), F32)
        for k in range(top):
            hit = routes[k : k + 1, :] == ids
            member = jnp.where(hit, 1.0, member)
            gate = jnp.where(hit, gates[k : k + 1, :], gate)
        rank = jnp.dot(member.astype(BF), upper, preferred_element_type=F32)
        rank = jnp.where(member > 0.0, rank, -1.0)
        pick = rank[:, None, :] == places
        weight = jnp.sum(jnp.where(pick, gate[:, None, :], 0.0), axis=2, keepdims=True)
        pick = jnp.where(pick, 1.0, 0.0).reshape(members * cap, toks).astype(BF)
        rows = jnp.dot(pick, rows_ref[:toks, :], preferred_element_type=F32)
        rows = (rows * weight.reshape(members * cap, 1)).astype(BF)
        out_ref[:, pl.ds(at, 1), :, :] = rows.reshape(members, 1, cap, width)


def dispatch(side, own_meta, got_meta, own, got, toks, experts, cap):
    width = own.shape[1]
    shape = (experts // 2, 2, cap, width)
    size = experts * cap * width

    def kernel(*refs):
        dispatch_kernel(toks, *refs)

    return pl.pallas_call(
        kernel,
        out_shape=jax.ShapeDtypeStruct(shape, BF),
        in_specs=[SM, VM, VM, VM, VM],
        out_specs=VM,
        name="dispatch",
        cost_estimate=cost(2 * size * toks, size * 2),
    )(side, own_meta, got_meta, own, got)


def hidden_kernel(half_ref, own_ref, other_ref, *refs):
    row_refs, out_ref = refs[:-1], refs[-1]
    run = out_ref.shape[0]
    cap = run // (2 * SHARE)

    def product(weight_ref):
        total = None
        at = 0
        for row_ref in row_refs:
            width = row_ref.shape[1]
            term = jnp.dot(
                row_ref[...], weight_ref[at : at + width, :], preferred_element_type=F32
            )
            total = term if total is None else total + term
            at += width
        total = total.astype(BF)
        for a in range(SHARE):
            for b in range(2):
                source, target = (a * 2 + b) * cap, (b * SHARE + a) * cap
                out_ref[target : target + cap, :] = total[source : source + cap, :]

    @pl.when(pl.program_id(1) == 0)
    def _():
        product(own_ref)

    @pl.when(pl.program_id(1) == 1)
    def _():
        product(other_ref)


def hidden(half, own, other, rows, cap):
    slots = rows[0].shape[0]
    d, half_rows = own.shape
    block = 2 * SHARE * cap
    return pl.pallas_call(
        hidden_kernel,
        grid_spec=pltpu.PrefetchScalarGridSpec(
            num_scalar_prefetch=1,
            grid=(slots // block, 2),
            in_specs=[pl.BlockSpec((d, half_rows), lambda i, j, h: (0, 0))] * 2
            + [pl.BlockSpec((block, r.shape[1]), lambda i, j, h: (i, 0)) for r in rows],
            out_specs=pl.BlockSpec(
                (block, half_rows), lambda i, j, h: (i, h[0] + j - 2 * h[0] * j)
            ),
        ),
        out_shape=jax.ShapeDtypeStruct((slots, 2 * half_rows), BF),
        name="hidden",
        cost_estimate=cost(4 * slots * half_rows * d, slots * d * 2 + slots * half_rows * 4),
    )(half, own, other, *rows)


def partner(block):
    count = lax.axis_size("pipe")
    route = [(i, (i + count // 2) % count) for i in range(count)]
    return lax.ppermute(block, "pipe", route)


def share(block):
    count = lax.axis_size("expert")
    return lax.ppermute(block, "expert", [(i, i ^ SHARE) for i in range(count)])


ROWS_ROWS = (((0,), (0,)), ((), ()))


def on_device(out_grad, gate_weights, routes, hidden_act, down_weight, block_scales):
    experts = lax.axis_size("expert")
    grad = out_grad[0, 0]
    toks = grad.shape[0]
    cap = toks * routes.shape[3] // experts
    slots = experts * cap
    upper = (lax.axis_index("pipe") >= lax.axis_size("pipe") // 2).astype(jnp.int32)
    side = ((lax.axis_index("expert") // SHARE) % 2).astype(jnp.int32).reshape(1)
    groups = [[i for i in range(experts) if (i & SHARE) == s] for s in (0, SHARE)]

    own = pack(routes[0, 0].T, gate_weights[0, 0].T, grad)
    got = []
    for block in own:
        got.append(share(block))
    own_half = dequantize(down_weight[0, 0], block_scales[0, 0])
    other_half = partner(own_half)

    act = hidden_act[0, 0, 0]
    ff = act.shape[1]
    act = act.reshape(-1, 2, SHARE, cap, ff).transpose(0, 2, 1, 3, 4).reshape(slots, ff)
    act_kept = lax.dynamic_slice_in_dim(act, upper * (ff // 2), ff // 2, 1)
    act_sent = lax.dynamic_slice_in_dim(act, (1 - upper) * (ff // 2), ff // 2, 1)

    rows, sent, kept = [], [], []
    for c in range(CHUNKS):
        block = dispatch(side, own[0], got[0], own[c], got[c], toks, experts, cap)
        block = lax.all_to_all(
            block, "expert", 0, 0, tiled=True, axis_index_groups=groups
        ).reshape(slots, -1)
        rows.append(block)
        part = lax.dot_general(act_sent, block, ROWS_ROWS, preferred_element_type=F32)
        sent.append(partner(part.astype(BF)))
        part = lax.dot_general(act_kept, block, ROWS_ROWS, preferred_element_type=F32)
        kept.append(lax.optimization_barrier(part.astype(BF)))
    hidden_grad = hidden(upper.reshape(1), own_half, other_half, rows, cap)
    weight_grad = jnp.concatenate(
        [(a.astype(F32) + b.astype(F32)).astype(BF) for a, b in zip(kept, sent)], axis=1
    )
    return hidden_grad[None, None, None], weight_grad[None, None]


def solution(mesh):
    row = P("pipe", None, "expert", None)
    in_specs = (
        row,
        row,
        row,
        P("pipe", None, "expert", None, None),
        P("pipe", "expert", None, None),
        P("pipe", "expert", None, None),
    )
    out_specs = (P("pipe", None, "expert", None, None), P("pipe", "expert", None, None))

    return jax.shard_map(
        on_device, mesh=mesh, in_specs=in_specs, out_specs=out_specs, check_vma=False
    )
```

time: 148 us -> 135 us (0.912)
  the two profiles are of different devices: /device:TPU:140 before, /device:TPU:1 now
where the time goes in v2:
time: 135 us; the launch traced here: 134 us
  starting transfers between devices  54.8 us (41%)
  waiting for transfers between devices  48.4 us (36%)
  Pallas kernels  20.9 us (15%)
  matrix products  5.11 us (4%)
  local copies, waits for them, and re-layouts  2.4 us (2%)
  other arithmetic  1.95 us (1%)
    all_to_all x2, waiting for transfers between devices, on_device(): lax.all_to_all(block, 'expert', 0, 0, tiled=True, axis_index_groups=groups)  25.3 us
    ppermute x3, starting transfers between devices, partner(): return lax.ppermute(block, 'pipe', route)  22.9 us
    all_to_all x2, starting transfers between devices, on_device(): lax.all_to_all(block, 'expert', 0, 0, tiled=True, axis_index_groups=groups)  19.9 us
    ppermute x3, waiting for transfers between devices, partner(): return lax.ppermute(block, 'pipe', route)  14.7 us
    ppermute x2, starting transfers between devices, share(): return lax.ppermute(block, 'expert', [(i, i ^ SHARE) for i in range(count)])  12.1 us
    pallas_call x1, Pallas kernels, hidden(): pl.pallas_call(hidden_kernel, grid_spec=pltpu.PrefetchScalarGridSpec(num_...  11.3 us
    ppermute x2, waiting for transfers between devices, share(): return lax.ppermute(block, 'expert', [(i, i ^ SHARE) for i in range(count)])  8.45 us
    pallas_call x2, Pallas kernels, dispatch(): pl.pallas_call(kernel, out_shape=jax.ShapeDtypeStruct(shape, BF), in_spec...  5.66 us
  transfers between devices with their start and end apart: 7, of which 5 were waited for; matrix products, arithmetic and copies ran while one was open for 5% of the time, Pallas kernels for 12%

profile of v2, /device:TPU:1, one launch (start us, length us, event | category | flops | bytes accessed | tf_op | source)
XLA Modules:
  0.0 134.4 jit_solution(6872616240267612264)
XLA Ops:
  0.6 1.7 %pack.1 = (bf16[144,512]{1,0:T(8,128)(2,1)}, bf16[128,512]{1,0:T(8,128)(2,1)}) custom-call(s32[8,128]{1,0:T(8,128)} %bitcast.38, f32[8,128]{1,0:T(8,128)} %bitcast.39, bf16[128,1024]{1,0:T(8,128)(2,1)} %bitcast.37), custom_call_target="tpu_custom_call" | custom-call | flops 131072 | bytes 524288 | tf_op jit(solution)/shard_map/pack/pallas_call | solution.py:65
  2.3 8.4 %collective-permute-start.1 = (bf16[144,512]{1,0:T(8,128)(2,1)}, bf16[144,512]{1,0:T(8,128)(2,1)S(1)}, u32[]{:S(2)}, u32[]{:S(2)}) collective-permute-start(bf16[144,512]{1,0:T(8,128)(2,1)} %get-tuple-element.4.refs_1_.refs_3_), channel_id=1, source_target_pairs={{0,4},{1,5},{2,6},{3,7},{4,0},{5,1},{6,2},{7,3},{8,12},{9,13},{10,... | collective-permute-start | bytes 442376 | tf_op jit(solution)/shard_map/ppermute | solution.py:182
  10.8 2.7 %collective-permute-done.1.refs_2_.refs_4_ = bf16[144,512]{1,0:T(8,128)(2,1)S(1)} collective-permute-done((bf16[144,512]{1,0:T(8,128)(2,1)}, bf16[144,512]{1,0:T(8,128)(2,1)S(1)}, u32[]{:S(2)}, u32[]{:S(2)}) %collective-permute-start.1) | collective-permute-done | bytes 147488 | tf_op jit(solution)/shard_map/ppermute | solution.py:182
  13.5 0.0 copy-start.2
  13.5 0.7 copy-done.2
  14.2 2.8 %dispatch.2 = bf16[32,2,16,512]{3,2,1,0:T(8,128)(2,1)} custom-call(s32[1]{0:T(128)} %bitcast.3.refs_0_, bf16[144,512]{1,0:T(8,128)(2,1)} %get-tuple-element.4.refs_1_.refs_3_, bf16[144,512]{1,0:T(8,128)(2,1)} %copy-done.2, bf16[144,512]{1,0:T(8,128)(2,1)} %get-tuple-element.4.refs_1_.refs_3_, bf16[144,512]{1,0:T(8,128)(2,1)} %copy-done.2), custom_call_target="tpu_custom_call" | custom-call | flops 134217728 | bytes 1048576 | tf_op jit(solution)/shard_map/dispatch/pallas_call | solution.py:113
  17.0 0.0 copy-start.6
  17.0 14.8 %all-to-all-start = ((bf16[32,2,16,512]{3,2,1,0:T(8,128)(2,1)}), bf16[32,2,16,512]{3,2,1,0:T(8,128)(2,1)S(1)}, u32[]{:S(2)}, u32[]{:S(2)}) async-start(bf16[32,2,16,512]{3,2,1,0:T(8,128)(2,1)} %dispatch.2), calls=%async_computation | async-start | bytes 2097152 | tf_op jit(solution)/shard_map/all_to_all | solution.py:214
  31.8 0.0 copy-done.6
  31.8 3.6 %collective-permute-start.2 = (bf16[128,512]{1,0:T(8,128)(2,1)S(1)}, bf16[128,512]{1,0:T(8,128)(2,1)S(1)}, u32[]{:S(2)}, u32[]{:S(2)}) collective-permute-start(bf16[128,512]{1,0:T(8,128)(2,1)S(1)} %copy-done.6), channel_id=1, source_target_pairs={{0,4},{1,5},{2,6},{3,7},{4,0},{5,1},{6,2},{7,3},{8,12},{9,13},{10,... | collective-permute-start | bytes 393224 | tf_op jit(solution)/shard_map/ppermute | solution.py:182
  35.5 5.8 %collective-permute-done.2.refs_4_ = bf16[128,512]{1,0:T(8,128)(2,1)S(1)} collective-permute-done((bf16[128,512]{1,0:T(8,128)(2,1)S(1)}, bf16[128,512]{1,0:T(8,128)(2,1)S(1)}, u32[]{:S(2)}, u32[]{:S(2)}) %collective-permute-start.2) | collective-permute-done | bytes 131104 | tf_op jit(solution)/shard_map/ppermute | solution.py:182
  41.2 0.0 copy-start.7
  41.2 0.6 copy-done.7
  41.9 2.8 %dispatch.3 = bf16[32,2,16,512]{3,2,1,0:T(8,128)(2,1)} custom-call(s32[1]{0:T(128)} %bitcast.3.refs_0_, bf16[144,512]{1,0:T(8,128)(2,1)} %get-tuple-element.4.refs_1_.refs_3_, bf16[144,512]{1,0:T(8,128)(2,1)} %copy-done.2, bf16[128,512]{1,0:T(8,128)(2,1)} %get-tuple-element.5.refs_3_, bf16[128,512]{1,0:T(8,128)(2,1)} %copy-done.7), custom_call_target="tpu_custom_call" | custom-call | flops 134217728 | bytes 1048576 | tf_op jit(solution)/shard_map/dispatch/pallas_call | solution.py:113
  44.7 15.1 %all-to-all-done = bf16[32,2,16,512]{3,2,1,0:T(8,128)(2,1)S(1)} async-done(((bf16[32,2,16,512]{3,2,1,0:T(8,128)(2,1)}), bf16[32,2,16,512]{3,2,1,0:T(8,128)(2,1)S(1)}, u32[]{:S(2)}, u32[]{:S(2)}) %all-to-all-start) | async-done | bytes 1048608 | tf_op jit(solution)/shard_map/all_to_all | solution.py:214
  59.8 0.0 copy-start
  59.8 5.1 %all-to-all-start.1 = ((bf16[32,2,16,512]{3,2,1,0:T(8,128)(2,1)}), bf16[32,2,16,512]{3,2,1,0:T(8,128)(2,1)S(1)}, u32[]{:S(2)}, u32[]{:S(2)}) async-start(bf16[32,2,16,512]{3,2,1,0:T(8,128)(2,1)} %dispatch.3), calls=%async_computation.1 | async-start | bytes 2097152 | tf_op jit(solution)/shard_map/all_to_all | solution.py:214
  64.9 0.0 copy-start.3
  65.0 2.1 %dequant.1.own_ref = bf16[1024,256]{1,0:T(8,128)(2,1)} custom-call(f32[2,8]{1,0:T(2,128)} %bitcast.40, bf16[256,1024]{1,0:T(8,128)(2,1)} %bitcast.36), custom_call_target="tpu_custom_call" | custom-call | flops 262144 | bytes 1048576 | tf_op jit(solution)/shard_map/dequant/pallas_call | solution.py:31
  67.1 10.5 %collective-permute-start = (bf16[1024,256]{1,0:T(8,128)(2,1)}, bf16[1024,256]{1,0:T(8,128)(2,1)}, u32[]{:S(2)}, u32[]{:S(2)}) collective-permute-start(bf16[1024,256]{1,0:T(8,128)(2,1)} %dequant.1.own_ref), channel_id=1, source_target_pairs={{0,512},{64,576},{128,640},{192,704},{256,768},{320,832},{384,896}... | collective-permute-start | bytes 1572872 | tf_op jit(solution)/shard_map/ppermute | solution.py:177
  77.6 0.0 copy-done.3
  77.6 1.1 copy.8
  78.7 0.0 copy-start.4
  78.7 2.3 %convolution_convert_fusion.2 = bf16[256,512]{1,0:T(8,128)(2,1)} fusion(bf16[1024,512]{1,0:T(8,128)(2,1)S(1)} %bitcast.24, bf16[1024,512]{1,0:T(8,128)(2,1)} %bitcast.32, s32[]{:T(128)S(6)} %select_n.17), kind=kOutput, calls=%fused_computation.2 | convolution fusion | flops 268566528 | bytes 1835012 | tf_op jit(solution)/shard_map/dot_general | solution.py:218
  81.0 1.9 %collective-permute-start.3 = (bf16[256,512]{1,0:T(8,128)(2,1)}, bf16[256,512]{1,0:T(8,128)(2,1)S(1)}, u32[]{:S(2)}, u32[]{:S(2)}) collective-permute-start(bf16[256,512]{1,0:T(8,128)(2,1)} %convolution_convert_fusion.2), channel_id=1, source_target_pairs={{0,512},{64,576},{128,640},{192,704},{256,768},{320,832},{384,896}... | collective-permute-start | bytes 786440 | tf_op jit(solution)/shard_map/ppermute | solution.py:177
  82.9 10.2 %all-to-all-done.1 = bf16[32,2,16,512]{3,2,1,0:T(8,128)(2,1)S(1)} async-done(((bf16[32,2,16,512]{3,2,1,0:T(8,128)(2,1)}), bf16[32,2,16,512]{3,2,1,0:T(8,128)(2,1)S(1)}, u32[]{:S(2)}, u32[]{:S(2)}) %all-to-all-start.1) | async-done | bytes 1048608 | tf_op jit(solution)/shard_map/all_to_all | solution.py:214
  93.1 0.0 copy-start.1
  93.1 0.0 copy-done.4
  93.1 1.2 convolution_convert_fusion
  94.2 10.5 %collective-permute-start.4 = (bf16[256,512]{1,0:T(8,128)(2,1)}, bf16[256,512]{1,0:T(8,128)(2,1)}, u32[]{:S(2)}, u32[]{:S(2)}) collective-permute-start(bf16[256,512]{1,0:T(8,128)(2,1)} %convolution_convert_fusion), channel_id=1, source_target_pairs={{0,512},{64,576},{128,640},{192,704},{256,768},{320,832},{384,896}... | collective-permute-start | bytes 786440 | tf_op jit(solution)/shard_map/ppermute | solution.py:177
  104.7 0.0 copy-done
  104.7 1.2 convolution_convert_fusion.3
  105.9 0.0 copy-done.1
  105.9 0.5 convolution_convert_fusion.1
  106.4 0.0 collective-permute-done.other_ref
  106.4 0.0 copy-start.5
  106.4 11.3 %hidden.1 = bf16[1024,512]{1,0:T(8,128)(2,1)} custom-call(s32[1]{0:T(128)} %bitcast.half_ref, bf16[1024,256]{1,0:T(8,128)(2,1)} %dequant.1.own_ref, bf16[1024,256]{1,0:T(8,128)(2,1)} %collective-permute-done.other_ref, bf16[1024,512]{1,0:T(8,128)(2,1)} %bitcast.26, bf16[1024,512]{1,0:T(8,128)(2,1)} %bitcast.29), custom_call_target="tpu_custom_call" | custom-call | flops 1073741824 | bytes 3145728 | tf_op jit(solution)/shard_map/hidden/pallas_call | solution.py:157
  117.7 0.0 collective-permute-done.3
  117.7 0.0 copy-done.5
  117.7 0.1 add_convert_fusion.1
  117.8 14.7 %collective-permute-done.4 = bf16[256,512]{1,0:T(8,128)(2,1)} collective-permute-done((bf16[256,512]{1,0:T(8,128)(2,1)}, bf16[256,512]{1,0:T(8,128)(2,1)}, u32[]{:S(2)}, u32[]{:S(2)}) %collective-permute-start.4) | collective-permute-done | bytes 262176 | tf_op jit(solution)/shard_map/ppermute | solution.py:177
  132.5 1.0 add_convert_fusion
  133.5 0.9 maximum_bitcast_fusion
Async XLA Ops:
  2.3 11.2 %collective-permute-start.1 = (bf16[144,512]{1,0:T(8,128)(2,1)}, bf16[144,512]{1,0:T(8,128)(2,1)S(1)}, u32[]{:S(2)}, u32[]{:S(2)}) collective-permute-start(bf16[144,512]{1,0:T(8,128)(2,1)} %get-tuple-element.4.refs_1_.refs_3_), channel_id=1, source_target_pairs={{0,4},{1,5},{2,6},{3,7},{4,0},{5,1},{6,2},{7,3},{8,12},{9,13},{10,... | collective-permute-start | bytes 442376 | tf_op jit(solution)/shard_map/ppermute | solution.py:182
  13.5 0.7 copy-start.2
  17.0 14.8 %copy-start.6 = (bf16[128,512]{1,0:T(8,128)(2,1)S(1)}, bf16[128,512]{1,0:T(8,128)(2,1)}, u32[]{:S(2)}) copy-start(bf16[128,512]{1,0:T(8,128)(2,1)} %get-tuple-element.5.refs_3_) | copy-start | bytes 393220
  17.0 42.8 %all-to-all-start = ((bf16[32,2,16,512]{3,2,1,0:T(8,128)(2,1)}), bf16[32,2,16,512]{3,2,1,0:T(8,128)(2,1)S(1)}, u32[]{:S(2)}, u32[]{:S(2)}) async-start(bf16[32,2,16,512]{3,2,1,0:T(8,128)(2,1)} %dispatch.2), calls=%async_computation | async-start | bytes 2097152 | tf_op jit(solution)/shard_map/all_to_all | solution.py:214
  31.8 9.4 %collective-permute-start.2 = (bf16[128,512]{1,0:T(8,128)(2,1)S(1)}, bf16[128,512]{1,0:T(8,128)(2,1)S(1)}, u32[]{:S(2)}, u32[]{:S(2)}) collective-permute-start(bf16[128,512]{1,0:T(8,128)(2,1)S(1)} %copy-done.6), channel_id=1, source_target_pairs={{0,4},{1,5},{2,6},{3,7},{4,0},{5,1},{6,2},{7,3},{8,12},{9,13},{10,... | collective-permute-start | bytes 393224 | tf_op jit(solution)/shard_map/ppermute | solution.py:182
  41.2 0.6 copy-start.7
  59.8 44.9 %copy-start = (bf16[32,2,16,512]{3,2,1,0:T(8,128)(2,1)}, bf16[32,2,16,512]{3,2,1,0:T(8,128)(2,1)S(1)}, u32[]{:S(2)}) copy-start(bf16[32,2,16,512]{3,2,1,0:T(8,128)(2,1)S(1)} %all-to-all-done) | copy-start | bytes 3145732
  59.8 33.2 %all-to-all-start.1 = ((bf16[32,2,16,512]{3,2,1,0:T(8,128)(2,1)}), bf16[32,2,16,512]{3,2,1,0:T(8,128)(2,1)S(1)}, u32[]{:S(2)}, u32[]{:S(2)}) async-start(bf16[32,2,16,512]{3,2,1,0:T(8,128)(2,1)} %dispatch.3), calls=%async_computation.1 | async-start | bytes 2097152 | tf_op jit(solution)/shard_map/all_to_all | solution.py:214
  64.9 12.7 %copy-start.3 = (bf16[1,1,1,1024,512]{4,3,2,1,0:T(8,128)(2,1)S(1)}, bf16[1,1,1,1024,512]{4,3,2,1,0:T(8,128)(2,1)}, u32[]{:S(2)}) copy-start(bf16[1,1,1,1024,512]{4,3,2,1,0:T(8,128)(2,1)} %param.9) | copy-start | bytes 3145732
  67.1 39.3 %collective-permute-start = (bf16[1024,256]{1,0:T(8,128)(2,1)}, bf16[1024,256]{1,0:T(8,128)(2,1)}, u32[]{:S(2)}, u32[]{:S(2)}) collective-permute-start(bf16[1024,256]{1,0:T(8,128)(2,1)} %dequant.1.own_ref), channel_id=1, source_target_pairs={{0,512},{64,576},{128,640},{192,704},{256,768},{320,832},{384,896}... | collective-permute-start | bytes 1572872 | tf_op jit(solution)/shard_map/ppermute | solution.py:177
  78.7 14.4 %copy-start.4 = (bf16[8,4,2,16,512]{4,3,2,1,0:T(8,128)(2,1)S(1)}, bf16[8,4,2,16,512]{4,3,2,1,0:T(8,128)(2,1)}, u32[]{:S(2)}) copy-start(bf16[8,4,2,16,512]{4,3,2,1,0:T(8,128)(2,1)} %copy.8) | copy-start | bytes 3145732
  81.0 36.8 %collective-permute-start.3 = (bf16[256,512]{1,0:T(8,128)(2,1)}, bf16[256,512]{1,0:T(8,128)(2,1)S(1)}, u32[]{:S(2)}, u32[]{:S(2)}) collective-permute-start(bf16[256,512]{1,0:T(8,128)(2,1)} %convolution_convert_fusion.2), channel_id=1, source_target_pairs={{0,512},{64,576},{128,640},{192,704},{256,768},{320,832},{384,896}... | collective-permute-start | bytes 786440 | tf_op jit(solution)/shard_map/ppermute | solution.py:177
  93.1 12.8 %copy-start.1 = (bf16[32,2,16,512]{3,2,1,0:T(8,128)(2,1)}, bf16[32,2,16,512]{3,2,1,0:T(8,128)(2,1)S(1)}, u32[]{:S(2)}) copy-start(bf16[32,2,16,512]{3,2,1,0:T(8,128)(2,1)S(1)} %all-to-all-done.1) | copy-start | bytes 3145732
  94.2 38.3 %collective-permute-start.4 = (bf16[256,512]{1,0:T(8,128)(2,1)}, bf16[256,512]{1,0:T(8,128)(2,1)}, u32[]{:S(2)}, u32[]{:S(2)}) collective-permute-start(bf16[256,512]{1,0:T(8,128)(2,1)} %convolution_convert_fusion), channel_id=1, source_target_pairs={{0,512},{64,576},{128,640},{192,704},{256,768},{320,832},{384,896}... | collective-permute-start | bytes 786440 | tf_op jit(solution)/shard_map/ppermute | solution.py:177
  106.4 11.4 %copy-start.5 = (bf16[256,512]{1,0:T(8,128)(2,1)S(1)}, bf16[256,512]{1,0:T(8,128)(2,1)}, u32[]{:S(2)}) copy-start(bf16[256,512]{1,0:T(8,128)(2,1)} %convolution_convert_fusion.3) | copy-start | bytes 786436

commit v3 on v2

--- a/solution.py
+++ b/solution.py
@@ -120,57 +120,6 @@
     )(side, own_meta, got_meta, own, got)
 
 
-def hidden_kernel(half_ref, own_ref, other_ref, *refs):
-    row_refs, out_ref = refs[:-1], refs[-1]
-    run = out_ref.shape[0]
-    cap = run // (2 * SHARE)
-
-    def product(weight_ref):
-        total = None
-        at = 0
-        for row_ref in row_refs:
-            width = row_ref.shape[1]
-            term = jnp.dot(
-                row_ref[...], weight_ref[at : at + width, :], preferred_element_type=F32
-            )
-            total = term if total is None else total + term
-            at += width
-        total = total.astype(BF)
-        for a in range(SHARE):
-            for b in range(2):
-                source, target = (a * 2 + b) * cap, (b * SHARE + a) * cap
-                out_ref[target : target + cap, :] = total[source : source + cap, :]
-
-    @pl.when(pl.program_id(1) == 0)
-    def _():
-        product(own_ref)
-
-    @pl.when(pl.program_id(1) == 1)
-    def _():
-        product(other_ref)
-
-
-def hidden(half, own, other, rows, cap):
-    slots = rows[0].shape[0]
-    d, half_rows = own.shape
-    block = 2 * SHARE * cap
-    return pl.pallas_call(
-        hidden_kernel,
-        grid_spec=pltpu.PrefetchScalarGridSpec(
-            num_scalar_prefetch=1,
-            grid=(slots // block, 2),
-            in_specs=[pl.BlockSpec((d, half_rows), lambda i, j, h: (0, 0))] * 2
-            + [pl.BlockSpec((block, r.shape[1]), lambda i, j, h: (i, 0)) for r in rows],
-            out_specs=pl.BlockSpec(
-                (block, half_rows), lambda i, j, h: (i, h[0] + j - 2 * h[0] * j)
-            ),
-        ),
-        out_shape=jax.ShapeDtypeStruct((slots, 2 * half_rows), BF),
-        name="hidden",
-        cost_estimate=cost(4 * slots * half_rows * d, slots * d * 2 + slots * half_rows * 4),
-    )(half, own, other, *rows)
-
-
 def partner(block):
     count = lax.axis_size("pipe")
     route = [(i, (i + count // 2) % count) for i in range(count)]
@@ -195,7 +144,7 @@
     side = ((lax.axis_index("expert") // SHARE) % 2).astype(jnp.int32).reshape(1)
     groups = [[i for i in range(experts) if (i & SHARE) == s] for s in (0, SHARE)]
 
-    own = pack(routes[0, 0].T, gate_weights[0, 0].T, grad)
+    own = list(pack(routes[0, 0].T, gate_weights[0, 0].T, grad))
     got = []
     for block in own:
         got.append(share(block))
@@ -208,18 +157,33 @@
     act_kept = lax.dynamic_slice_in_dim(act, upper * (ff // 2), ff // 2, 1)
     act_sent = lax.dynamic_slice_in_dim(act, (1 - upper) * (ff // 2), ff // 2, 1)
 
-    rows, sent, kept = [], [], []
+    total, at = None, 0
+    sent, kept = [], []
     for c in range(CHUNKS):
+        if c == 1:
+            own[c], act_kept, act_sent = lax.optimization_barrier((own[c], act_kept, act_sent))
         block = dispatch(side, own[0], got[0], own[c], got[c], toks, experts, cap)
         block = lax.all_to_all(
             block, "expert", 0, 0, tiled=True, axis_index_groups=groups
         ).reshape(slots, -1)
-        rows.append(block)
         part = lax.dot_general(act_sent, block, ROWS_ROWS, preferred_element_type=F32)
-        sent.append(partner(part.astype(BF)))
+        part = part.astype(BF)
+        if c == 0:
+            _, other_half = lax.optimization_barrier((part, other_half))
+            whole = jnp.where(
+                upper == 1,
+                jnp.concatenate([other_half, own_half], axis=1),
+                jnp.concatenate([own_half, other_half], axis=1),
+            )
+        sent.append(partner(part))
         part = lax.dot_general(act_kept, block, ROWS_ROWS, preferred_element_type=F32)
         kept.append(lax.optimization_barrier(part.astype(BF)))
-    hidden_grad = hidden(upper.reshape(1), own_half, other_half, rows, cap)
+        width = block.shape[1]
+        part = jnp.dot(block, whole[at : at + width], preferred_element_type=F32)
+        total = part if total is None else total + part
+        at += width
+    hidden_grad = total.astype(BF).reshape(-1, SHARE, 2, cap, ff)
+    hidden_grad = hidden_grad.transpose(0, 2, 1, 3, 4).reshape(slots, ff)
     weight_grad = jnp.concatenate(
         [(a.astype(F32) + b.astype(F32)).astype(BF) for a, b in zip(kept, sent)], axis=1
     )

time: 135 us -> 131 us (0.970)
  the two profiles are of different devices: /device:TPU:1 before, /device:TPU:260 now
where the time goes in v3:
time: 131 us; the launch traced here: 130 us
  waiting for transfers between devices  70.7 us (54%)
  starting transfers between devices  37.5 us (29%)
  Pallas kernels  9.48 us (7%)
  matrix products  6.71 us (5%)
  local copies, waits for them, and re-layouts  3.84 us (3%)
    ppermute x3, waiting for transfers between devices, partner(): return lax.ppermute(block, 'pipe', route)  41.8 us
    ppermute x3, starting transfers between devices, partner(): return lax.ppermute(block, 'pipe', route)  17.8 us
    ppermute x2, waiting for transfers between devices, share(): return lax.ppermute(block, 'expert', [(i, i ^ SHARE) for i in range(count)])  16.1 us
    all_to_all x2, starting transfers between devices, on_device(): lax.all_to_all(block, 'expert', 0, 0, tiled=True, axis_index_groups=groups)  15.7 us
    all_to_all x2, waiting for transfers between devices, on_device(): lax.all_to_all(block, 'expert', 0, 0, tiled=True, axis_index_groups=groups)  12.8 us
    pallas_call x2, Pallas kernels, dispatch(): pl.pallas_call(kernel, out_shape=jax.ShapeDtypeStruct(shape, BF), in_spec...  5.63 us
    ppermute x2, starting transfers between devices, share(): return lax.ppermute(block, 'expert', [(i, i ^ SHARE) for i in range(count)])  3.96 us
    dot_general x2, matrix products, on_device(): lax.dot_general(act_sent, block, ROWS_ROWS, preferred_element_type=F32)  2.66 us
  transfers between devices with their start and end apart: 7, of which 5 were waited for; matrix products, arithmetic and copies ran while one was open for 7% of the time, Pallas kernels for 4%

profile of v3, /device:TPU:260, one launch (start us, length us, event | category | flops | bytes accessed | tf_op | source)
XLA Modules:
  0.0 130.3 jit_solution(16566113652559898682)
XLA Ops:
  0.6 0.0 copy-start.2
  0.6 1.8 %pack.1 = (bf16[144,512]{1,0:T(8,128)(2,1)}, bf16[128,512]{1,0:T(8,128)(2,1)}) custom-call(s32[8,128]{1,0:T(8,128)} %bitcast.44, f32[8,128]{1,0:T(8,128)} %bitcast.45, bf16[128,1024]{1,0:T(8,128)(2,1)} %bitcast.43), custom_call_target="tpu_custom_call" | custom-call | flops 131072 | bytes 524288 | tf_op jit(solution)/shard_map/pack/pallas_call | solution.py:65
  2.4 0.0 copy-start.6
  2.4 2.0 %collective-permute-start = (bf16[144,512]{1,0:T(8,128)(2,1)}, bf16[144,512]{1,0:T(8,128)(2,1)S(1)}, u32[]{:S(2)}, u32[]{:S(2)}) collective-permute-start(bf16[144,512]{1,0:T(8,128)(2,1)} %get-tuple-element.8.refs_1_.refs_3_), channel_id=1, source_target_pairs={{0,4},{1,5},{2,6},{3,7},{4,0},{5,1},{6,2},{7,3},{8,12},{9,13},{10,... | collective-permute-start | bytes 442376 | tf_op jit(solution)/shard_map/ppermute | solution.py:131
  4.5 6.8 %collective-permute-done.refs_2_.refs_4_ = bf16[144,512]{1,0:T(8,128)(2,1)S(1)} collective-permute-done((bf16[144,512]{1,0:T(8,128)(2,1)}, bf16[144,512]{1,0:T(8,128)(2,1)S(1)}, u32[]{:S(2)}, u32[]{:S(2)}) %collective-permute-start) | collective-permute-done | bytes 147488 | tf_op jit(solution)/shard_map/ppermute | solution.py:131
  11.4 0.0 copy-start.1
  11.4 0.7 copy-done.1
  12.0 2.8 %dispatch.2 = bf16[32,2,16,512]{3,2,1,0:T(8,128)(2,1)} custom-call(s32[1]{0:T(128)} %bitcast.refs_0_, bf16[144,512]{1,0:T(8,128)(2,1)} %get-tuple-element.8.refs_1_.refs_3_, bf16[144,512]{1,0:T(8,128)(2,1)} %copy-done.1, bf16[144,512]{1,0:T(8,128)(2,1)} %get-tuple-element.8.refs_1_.refs_3_, bf16[144,512]{1,0:T(8,128)(2,1)} %copy-done.1), custom_call_target="tpu_custom_call" | custom-call | flops 134217728 | bytes 1048576 | tf_op jit(solution)/shard_map/dispatch/pallas_call | solution.py:113
  14.8 11.8 %all-to-all-start = ((bf16[32,2,16,512]{3,2,1,0:T(8,128)(2,1)}), bf16[32,2,16,512]{3,2,1,0:T(8,128)(2,1)S(1)}, u32[]{:S(2)}, u32[]{:S(2)}) async-start(bf16[32,2,16,512]{3,2,1,0:T(8,128)(2,1)} %dispatch.2), calls=%async_computation | async-start | bytes 2097152 | tf_op jit(solution)/shard_map/all_to_all | solution.py:166
  26.6 0.0 copy-done.6
  26.6 1.9 %collective-permute-start.2 = (bf16[128,512]{1,0:T(8,128)(2,1)S(1)}, bf16[128,512]{1,0:T(8,128)(2,1)S(1)}, u32[]{:S(2)}, u32[]{:S(2)}) collective-permute-start(bf16[128,512]{1,0:T(8,128)(2,1)S(1)} %copy-done.6), channel_id=1, source_target_pairs={{0,4},{1,5},{2,6},{3,7},{4,0},{5,1},{6,2},{7,3},{8,12},{9,13},{10,... | collective-permute-start | bytes 393224 | tf_op jit(solution)/shard_map/ppermute | solution.py:131
  28.6 0.0 copy-done.2
  28.6 0.1 copy.10
  28.7 1.1 constant_dynamic-slice_fusion.1
  29.8 0.0 copy-start.4
  29.8 9.2 %collective-permute-done.2.refs_4_ = bf16[128,512]{1,0:T(8,128)(2,1)S(1)} collective-permute-done((bf16[128,512]{1,0:T(8,128)(2,1)S(1)}, bf16[128,512]{1,0:T(8,128)(2,1)S(1)}, u32[]{:S(2)}, u32[]{:S(2)}) %collective-permute-start.2) | collective-permute-done | bytes 131104 | tf_op jit(solution)/shard_map/ppermute | solution.py:131
  39.0 0.0 copy-start.7
  39.0 0.6 copy-done.7
  39.6 2.8 %dispatch.3 = bf16[32,2,16,512]{3,2,1,0:T(8,128)(2,1)} custom-call(s32[1]{0:T(128)} %bitcast.refs_0_, bf16[144,512]{1,0:T(8,128)(2,1)} %get-tuple-element.8.refs_1_.refs_3_, bf16[144,512]{1,0:T(8,128)(2,1)} %copy-done.1, bf16[128,512]{1,0:T(8,128)(2,1)} %get-tuple-element.11.refs_3_, bf16[128,512]{1,0:T(8,128)(2,1)} %copy-done.7), custom_call_target="tpu_custom_call" | custom-call | flops 134217728 | bytes 1048576 | tf_op jit(solution)/shard_map/dispatch/pallas_call | solution.py:113
  42.4 12.8 %all-to-all-done = bf16[32,2,16,512]{3,2,1,0:T(8,128)(2,1)S(1)} async-done(((bf16[32,2,16,512]{3,2,1,0:T(8,128)(2,1)}), bf16[32,2,16,512]{3,2,1,0:T(8,128)(2,1)S(1)}, u32[]{:S(2)}, u32[]{:S(2)}) %all-to-all-start) | async-done | bytes 1048608 | tf_op jit(solution)/shard_map/all_to_all | solution.py:166
  55.2 3.9 %all-to-all-start.1 = ((bf16[32,2,16,512]{3,2,1,0:T(8,128)(2,1)}), bf16[32,2,16,512]{3,2,1,0:T(8,128)(2,1)S(1)}, u32[]{:S(2)}, u32[]{:S(2)}) async-start(bf16[32,2,16,512]{3,2,1,0:T(8,128)(2,1)} %dispatch.3), calls=%async_computation.1 | async-start | bytes 2097152 | tf_op jit(solution)/shard_map/all_to_all | solution.py:166
  59.2 2.1 %dequant.1 = bf16[1024,256]{1,0:T(8,128)(2,1)} custom-call(f32[2,8]{1,0:T(2,128)} %bitcast.46, bf16[256,1024]{1,0:T(8,128)(2,1)} %bitcast.42), custom_call_target="tpu_custom_call" | custom-call | flops 262144 | bytes 1048576 | tf_op jit(solution)/shard_map/dequant/pallas_call | solution.py:31
  61.2 12.7 %collective-permute-start.1 = (bf16[1024,256]{1,0:T(8,128)(2,1)}, bf16[1024,256]{1,0:T(8,128)(2,1)S(1)}, u32[]{:S(2)}, u32[]{:S(2)}) collective-permute-start(bf16[1024,256]{1,0:T(8,128)(2,1)} %dequant.1), channel_id=1, source_target_pairs={{0,512},{64,576},{128,640},{192,704},{256,768},{320,832},{384,896}... | collective-permute-start | bytes 1572872 | tf_op jit(solution)/shard_map/ppermute | solution.py:126
  74.0 0.0 copy-done.4
  74.0 1.2 convolution_convert_fusion.3
  75.2 0.0 copy-start
  75.2 2.0 %collective-permute-start.3 = (bf16[256,512]{1,0:T(8,128)(2,1)}, bf16[256,512]{1,0:T(8,128)(2,1)S(1)}, u32[]{:S(2)}, u32[]{:S(2)}) collective-permute-start(bf16[256,512]{1,0:T(8,128)(2,1)} %convolution_convert_fusion.3), channel_id=1, source_target_pairs={{0,512},{64,576},{128,640},{192,704},{256,768},{320,832},{384,896}... | collective-permute-start | bytes 786440 | tf_op jit(solution)/shard_map/ppermute | solution.py:126
  77.2 34.9 %collective-permute-done.1 = bf16[1024,256]{1,0:T(8,128)(2,1)S(1)} collective-permute-done((bf16[1024,256]{1,0:T(8,128)(2,1)}, bf16[1024,256]{1,0:T(8,128)(2,1)S(1)}, u32[]{:S(2)}, u32[]{:S(2)}) %collective-permute-start.1) | collective-permute-done | bytes 524320 | tf_op jit(solution)/shard_map/ppermute | solution.py:126
  112.1 2.2 %convolution_convert_fusion.2 = bf16[256,512]{1,0:T(8,128)(2,1)} fusion(bf16[1024,256]{1,0:T(8,128)(2,1)} %get-tuple-element.12, bf16[1024,512]{1,0:T(8,128)(2,1)S(1)} %bitcast.37), kind=kOutput, calls=%fused_computation.3 | convolution fusion | flops 268566528 | bytes 1835008 | tf_op jit(solution)/shard_map/dot_general | solution.py:179
  114.3 0.0 all-to-all-done.1
  114.3 1.5 %convolution_convert_fusion = bf16[256,512]{1,0:T(8,128)(2,1)S(1)} fusion(bf16[1024,256]{1,0:T(8,128)(2,1)} %get-tuple-element.13, bf16[1024,512]{1,0:T(8,128)(2,1)S(1)} %bitcast.32), kind=kOutput, calls=%fused_computation.1 | convolution fusion | flops 268566528 | bytes 1835008 | tf_op jit(solution)/shard_map/dot_general | solution.py:169
  115.8 3.0 %collective-permute-start.4 = (bf16[256,512]{1,0:T(8,128)(2,1)S(1)}, bf16[256,512]{1,0:T(8,128)(2,1)S(1)}, u32[]{:S(2)}, u32[]{:S(2)}) collective-permute-start(bf16[256,512]{1,0:T(8,128)(2,1)S(1)} %convolution_convert_fusion), channel_id=1, source_target_pairs={{0,512},{64,576},{128,640},{192,704},{256,768},{320,832},{384,896}... | collective-permute-start | bytes 786440 | tf_op jit(solution)/shard_map/ppermute | solution.py:126
  118.8 0.0 copy-done
  118.9 0.2 maximum_select_fusion
  119.1 0.7 fusion
  119.8 0.0 copy-start.3
  119.8 0.7 add_convert_fusion
  120.5 0.3 copy-done.3
  120.9 0.0 copy-start.5
  120.9 0.5 convolution_convert_fusion.1
  121.3 1.0 copy.11
  122.4 0.0 collective-permute-done.3
  122.4 0.0 copy-done.5
  122.4 0.1 add_convert_fusion.2
  122.4 6.9 %collective-permute-done.4 = bf16[256,512]{1,0:T(8,128)(2,1)S(1)} collective-permute-done((bf16[256,512]{1,0:T(8,128)(2,1)S(1)}, bf16[256,512]{1,0:T(8,128)(2,1)S(1)}, u32[]{:S(2)}, u32[]{:S(2)}) %collective-permute-start.4) | collective-permute-done | bytes 262176 | tf_op jit(solution)/shard_map/ppermute | solution.py:126
  129.4 0.1 add_convert_fusion.1
  129.4 0.9 maximum_bitcast_fusion
Async XLA Ops:
  0.6 28.0 %copy-start.2 = (bf16[1,1,1,1024,512]{4,3,2,1,0:T(8,128)(2,1)S(1)}, bf16[1,1,1,1024,512]{4,3,2,1,0:T(8,128)(2,1)}, u32[]{:S(2)}) copy-start(bf16[1,1,1,1024,512]{4,3,2,1,0:T(8,128)(2,1)} %param.9) | copy-start | bytes 3145732
  2.4 24.2 %copy-start.6 = (bf16[128,512]{1,0:T(8,128)(2,1)S(1)}, bf16[128,512]{1,0:T(8,128)(2,1)}, u32[]{:S(2)}) copy-start(bf16[128,512]{1,0:T(8,128)(2,1)} %get-tuple-element.11.refs_3_) | copy-start | bytes 393220
  2.4 8.9 %collective-permute-start = (bf16[144,512]{1,0:T(8,128)(2,1)}, bf16[144,512]{1,0:T(8,128)(2,1)S(1)}, u32[]{:S(2)}, u32[]{:S(2)}) collective-permute-start(bf16[144,512]{1,0:T(8,128)(2,1)} %get-tuple-element.8.refs_1_.refs_3_), channel_id=1, source_target_pairs={{0,4},{1,5},{2,6},{3,7},{4,0},{5,1},{6,2},{7,3},{8,12},{9,13},{10,... | collective-permute-start | bytes 442376 | tf_op jit(solution)/shard_map/ppermute | solution.py:131
  11.4 0.7 copy-start.1
  14.8 40.4 %all-to-all-start = ((bf16[32,2,16,512]{3,2,1,0:T(8,128)(2,1)}), bf16[32,2,16,512]{3,2,1,0:T(8,128)(2,1)S(1)}, u32[]{:S(2)}, u32[]{:S(2)}) async-start(bf16[32,2,16,512]{3,2,1,0:T(8,128)(2,1)} %dispatch.2), calls=%async_computation | async-start | bytes 2097152 | tf_op jit(solution)/shard_map/all_to_all | solution.py:166
  26.6 12.4 %collective-permute-start.2 = (bf16[128,512]{1,0:T(8,128)(2,1)S(1)}, bf16[128,512]{1,0:T(8,128)(2,1)S(1)}, u32[]{:S(2)}, u32[]{:S(2)}) collective-permute-start(bf16[128,512]{1,0:T(8,128)(2,1)S(1)} %copy-done.6), channel_id=1, source_target_pairs={{0,4},{1,5},{2,6},{3,7},{4,0},{5,1},{6,2},{7,3},{8,12},{9,13},{10,... | collective-permute-start | bytes 393224 | tf_op jit(solution)/shard_map/ppermute | solution.py:131
  29.8 44.2 %copy-start.4 = (bf16[1024,256]{1,0:T(8,128)(2,1)S(1)}, bf16[1024,256]{1,0:T(8,128)(2,1)}, u32[]{:S(2)}) copy-start(bf16[1024,256]{1,0:T(8,128)(2,1)} %get-tuple-element.13) | copy-start | bytes 1572868
  39.0 0.6 copy-start.7
  55.2 59.1 %all-to-all-start.1 = ((bf16[32,2,16,512]{3,2,1,0:T(8,128)(2,1)}), bf16[32,2,16,512]{3,2,1,0:T(8,128)(2,1)S(1)}, u32[]{:S(2)}, u32[]{:S(2)}) async-start(bf16[32,2,16,512]{3,2,1,0:T(8,128)(2,1)} %dispatch.3), calls=%async_computation.1 | async-start | bytes 2097152 | tf_op jit(solution)/shard_map/all_to_all | solution.py:166
  61.2 50.9 %collective-permute-start.1 = (bf16[1024,256]{1,0:T(8,128)(2,1)}, bf16[1024,256]{1,0:T(8,128)(2,1)S(1)}, u32[]{:S(2)}, u32[]{:S(2)}) collective-permute-start(bf16[1024,256]{1,0:T(8,128)(2,1)} %dequant.1), channel_id=1, source_target_pairs={{0,512},{64,576},{128,640},{192,704},{256,768},{320,832},{384,896}... | collective-permute-start | bytes 1572872 | tf_op jit(solution)/shard_map/ppermute | solution.py:126
  75.2 43.7 %copy-start = (bf16[1024,256]{1,0:T(8,128)(2,1)S(1)}, bf16[1024,256]{1,0:T(8,128)(2,1)}, u32[]{:S(2)}) copy-start(bf16[1024,256]{1,0:T(8,128)(2,1)} %dequant.1) | copy-start | bytes 1572868
  75.2 47.2 %collective-permute-start.3 = (bf16[256,512]{1,0:T(8,128)(2,1)}, bf16[256,512]{1,0:T(8,128)(2,1)S(1)}, u32[]{:S(2)}, u32[]{:S(2)}) collective-permute-start(bf16[256,512]{1,0:T(8,128)(2,1)} %convolution_convert_fusion.3), channel_id=1, source_target_pairs={{0,512},{64,576},{128,640},{192,704},{256,768},{320,832},{384,896}... | collective-permute-start | bytes 786440 | tf_op jit(solution)/shard_map/ppermute | solution.py:126
  115.8 13.6 %collective-permute-start.4 = (bf16[256,512]{1,0:T(8,128)(2,1)S(1)}, bf16[256,512]{1,0:T(8,128)(2,1)S(1)}, u32[]{:S(2)}, u32[]{:S(2)}) collective-permute-start(bf16[256,512]{1,0:T(8,128)(2,1)S(1)} %convolution_convert_fusion), channel_id=1, source_target_pairs={{0,512},{64,576},{128,640},{192,704},{256,768},{320,832},{384,896}... | collective-permute-start | bytes 786440 | tf_op jit(solution)/shard_map/ppermute | solution.py:126
  119.8 1.0 copy-start.3
  120.9 1.5 %copy-start.5 = (bf16[256,512]{1,0:T(8,128)(2,1)S(1)}, bf16[256,512]{1,0:T(8,128)(2,1)}, u32[]{:S(2)}) copy-start(bf16[256,512]{1,0:T(8,128)(2,1)} %convolution_convert_fusion.2) | copy-start | bytes 786436

commit v4 on v3

v4 whole, which is shorter than its diff:
```python
import jax
import jax.numpy as jnp
from jax import lax
from jax.experimental import pallas as pl
from jax.experimental.pallas import tpu as pltpu
from jax.sharding import PartitionSpec as P

QBLOCK = 128
RUN = 4
FIRST = 512
BF = jnp.bfloat16
F32 = jnp.float32
VM = pl.BlockSpec(memory_space=pltpu.VMEM)
SM = pl.BlockSpec(memory_space=pltpu.SMEM)


def cost(flops, nbytes):
    return pl.CostEstimate(flops=flops, bytes_accessed=nbytes, transcendentals=0)


def dequant_kernel(scale_ref, weight_ref, out_ref):
    rows, cols = weight_ref.shape
    for i in range(rows // QBLOCK):
        for j in range(cols // QBLOCK):
            here, there = pl.ds(i * QBLOCK, QBLOCK), pl.ds(j * QBLOCK, QBLOCK)
            block = weight_ref[here, there].astype(F32) * scale_ref[i, j]
            out_ref[there, here] = block.T.astype(BF)


def dequantize(weight, scales):
    return pl.pallas_call(
        dequant_kernel,
        out_shape=jax.ShapeDtypeStruct(weight.shape[::-1], BF),
        in_specs=[SM, VM],
        out_specs=VM,
        name="dequant",
        cost_estimate=cost(weight.size, weight.size * 4),
    )(scales, weight)


def pack_kernel(route_ref, gate_ref, grad_ref, out_ref):
    toks, width = grad_ref.shape
    top = route_ref.shape[0]
    gate = gate_ref[...]
    high = gate.astype(BF)
    left = gate - high.astype(F32)
    middle = left.astype(BF)
    low = (left - middle.astype(F32)).astype(BF)
    out_ref[:toks, :] = grad_ref[...]
    out_ref[toks:, :] = jnp.zeros((2 * top, width), BF)
    pairs = ((route_ref[...].astype(F32), high), (middle, low))
    for at, (a, b) in enumerate(pairs):
        both = jnp.concatenate([a.astype(F32), b.astype(F32)], axis=0)
        out_ref[toks:, at * toks : (at + 1) * toks] = both.astype(BF)


def whole_block(shape):
    return pl.BlockSpec(shape, lambda i: (0, 0))


def pack(routes, gates, grad):
    toks, d = grad.shape
    top = routes.shape[0]
    width = d - FIRST
    return pl.pallas_call(
        pack_kernel,
        grid=(1,),
        out_shape=jax.ShapeDtypeStruct((toks + 2 * top, width), BF),
        in_specs=[
            whole_block(routes.shape),
            whole_block(gates.shape),
            pl.BlockSpec((toks, width), lambda i: (0, FIRST // width)),
        ],
        out_specs=whole_block((toks + 2 * top, width)),
        name="pack",
        cost_estimate=cost(toks * width, toks * width * 4),
    )(routes, gates, grad)


def place(routes, gates, ids, cap):
    top, toks = routes.shape
    experts = ids.shape[0]
    member = jnp.zeros((experts, toks), F32)
    gate = jnp.zeros((experts, toks), F32)
    for k in range(top):
        hit = routes[k : k + 1, :] == ids
        member = jnp.where(hit, 1.0, member)
        gate = jnp.where(hit, gates[k : k + 1, :], gate)
    earlier = lax.broadcasted_iota(jnp.int32, (toks, toks), 0)
    later = lax.broadcasted_iota(jnp.int32, (toks, toks), 1)
    upper = jnp.where(earlier < later, 1.0, 0.0).astype(BF)
    rank = jnp.dot(member.astype(BF), upper, preferred_element_type=F32)
    rank = jnp.where(member > 0.0, rank, -1.0)
    places = lax.broadcasted_iota(jnp.int32, (experts, cap, toks), 1).astype(F32)
    pick = rank[:, None, :] == places
    weight = jnp.sum(jnp.where(pick, gate[:, None, :], 0.0), axis=2, keepdims=True)
    pick = jnp.where(pick, 1.0, 0.0).reshape(experts * cap, toks).astype(BF)
    return pick, weight.reshape(experts * cap, 1)


def direct_kernel(route_ref, gate_ref, grad_ref, out_ref):
    experts, cap, width = out_ref.shape
    toks = grad_ref.shape[0]
    ids = lax.broadcasted_iota(jnp.int32, (experts, toks), 0)
    pick, weight = place(route_ref[...], gate_ref[...], ids, cap)
    rows = jnp.dot(pick, grad_ref[...], preferred_element_type=F32)
    out_ref[...] = (rows * weight).astype(BF).reshape(experts, cap, width)


def dispatch_direct(routes, gates, grad, experts, cap):
    toks = grad.shape[0]
    size = experts * cap * FIRST
    return pl.pallas_call(
        direct_kernel,
        grid=(1,),
        out_shape=jax.ShapeDtypeStruct((experts, cap, FIRST), BF),
        in_specs=[
            whole_block(routes.shape),
            whole_block(gates.shape),
            whole_block((toks, FIRST)),
        ],
        out_specs=pl.BlockSpec((experts, cap, FIRST), lambda i: (0, 0, 0)),
        name="direct",
        cost_estimate=cost(2 * size * toks, size * 2),
    )(routes, gates, grad)


def shared_kernel(toks, where_ref, *refs):
    block_refs, out_ref = refs[:-1], refs[-1]
    members, _, cap, width = out_ref.shape
    side = where_ref[0]
    line = lax.broadcasted_iota(jnp.int32, (members, toks), 0)
    ids = (line // 2) * (2 * RUN) + side * 2 + line % 2
    for k, ref in enumerate(block_refs):
        meta = ref[toks:, : 2 * toks].astype(F32)
        top = meta.shape[0] // 2
        routes = meta[:top, :toks].astype(jnp.int32)
        gates = meta[top:, :toks] + (meta[:top, toks:] + meta[top:, toks:])
        pick, weight = place(routes, gates, ids, cap)
        rows = jnp.dot(pick, ref[:toks, :], preferred_element_type=F32)
        rows = (rows * weight).astype(BF).reshape(members, 1, cap, width)
        out_ref[:, pl.ds(side ^ k, 1), :, :] = rows


def dispatch_shared(side, blocks, toks, experts, cap):
    width = blocks[0].shape[1]
    shape = (experts // RUN, RUN, cap, width)
    size = experts * cap * width

    def kernel(*refs):
        shared_kernel(toks, *refs)

    return pl.pallas_call(
        kernel,
        out_shape=jax.ShapeDtypeStruct(shape, BF),
        in_specs=[SM] + [VM] * len(blocks),
        out_specs=VM,
        name="shared",
        cost_estimate=cost(2 * size * toks, size * 2),
    )(side, *blocks)


def partner(block):
    count = lax.axis_size("pipe")
    route = [(i, (i + count // 2) % count) for i in range(count)]
    return lax.ppermute(block, "pipe", route)


def share(block, k):
    count = lax.axis_size("expert")
    return lax.ppermute(block, "expert", [(i, i ^ (2 * k)) for i in range(count)])


ROWS_ROWS = (((0,), (0,)), ((), ()))


def on_device(out_grad, gate_weights, routes, hidden_act, down_weight, block_scales):
    experts = lax.axis_size("expert")
    grad = out_grad[0, 0]
    toks = grad.shape[0]
    cap = toks * routes.shape[3] // experts
    slots = experts * cap
    upper = (lax.axis_index("pipe") >= lax.axis_size("pipe") // 2).astype(jnp.int32)
    side = ((lax.axis_index("expert") // 2) % RUN).astype(jnp.int32).reshape(1)
    groups = [
        [i for i in range(experts) if i // 2 % RUN == z] for z in range(RUN)
    ]
    routes, gates = routes[0, 0].T, gate_weights[0, 0].T

    packed = pack(routes, gates, grad)
    blocks = [packed]
    for k in range(1, RUN):
        blocks.append(share(packed, k))
    own_half = dequantize(down_weight[0, 0], block_scales[0, 0])
    other_half = partner(own_half)

    act = hidden_act[0, 0, 0]
    ff = act.shape[1]

    def halves(x):
        keep = lax.dynamic_slice_in_dim(x, upper * (ff // 2), ff // 2, 1)
        send = lax.dynamic_slice_in_dim(x, (1 - upper) * (ff // 2), ff // 2, 1)
        return keep, send

    turned = act.reshape(-1, RUN, 2, cap, ff).transpose(0, 2, 1, 3, 4).reshape(slots, ff)
    pieces = [halves(act), halves(turned)]

    first = dispatch_direct(routes, gates, grad, experts, cap)
    first = lax.all_to_all(first, "expert", 0, 0, tiled=True).reshape(slots, -1)
    pieces, blocks[0] = lax.optimization_barrier((pieces, blocks[0]))
    second = dispatch_shared(side, blocks, toks, experts, cap)
    second = lax.all_to_all(
        second, "expert", 0, 0, tiled=True, axis_index_groups=groups
    ).reshape(slots, -1)

    sent, kept = [], []
    for (keep, send), rows in zip(pieces, (first, second)):
        part = lax.dot_general(send, rows, ROWS_ROWS, preferred_element_type=F32).astype(BF)
        sent.append(partner(part))
        part = lax.dot_general(keep, rows, ROWS_ROWS, preferred_element_type=F32)
        kept.append(lax.optimization_barrier(part.astype(BF)))
    whole = jnp.where(
        upper == 1,
        jnp.concatenate([other_half, own_half], axis=1),
        jnp.concatenate([own_half, other_half], axis=1),
    )
    width = second.shape[1]
    second = second.reshape(-1, 2, RUN, cap, width).transpose(0, 2, 1, 3, 4)
    second = second.reshape(slots, width)
    total = jnp.dot(first, whole[:FIRST], preferred_element_type=F32)
    total = total + jnp.dot(second, whole[FIRST:], preferred_element_type=F32)
    hidden_grad = total.astype(BF)
    sums = []
    for a, b in zip(kept, sent):
        sums.append((a.astype(F32) + b.astype(F32)).astype(BF))
    weight_grad = jnp.concatenate(sums, axis=1)
    return hidden_grad[None, None, None], weight_grad[None, None]


def solution(mesh):
    row = P("pipe", None, "expert", None)
    in_specs = (
        row,
        row,
        row,
        P("pipe", None, "expert", None, None),
        P("pipe", "expert", None, None),
        P("pipe", "expert", None, None),
    )
    out_specs = (P("pipe", None, "expert", None, None), P("pipe", "expert", None, None))

    return jax.shard_map(
        on_device, mesh=mesh, in_specs=in_specs, out_specs=out_specs, check_vma=False
    )
```

time: 131 us -> 144 us (1.099)
  the two profiles are of different devices: /device:TPU:260 before, /device:TPU:1 now
where the time goes in v4:
time: 144 us; the launch traced here: 143 us
  waiting for transfers between devices  63.8 us (44%)
  starting transfers between devices  54.7 us (38%)
  Pallas kernels  9.33 us (6%)
  matrix products  6.98 us (5%)
  local copies, waits for them, and re-layouts  3.96 us (3%)
  other arithmetic  3.73 us (3%)
    ppermute x3, waiting for transfers between devices, partner(): return lax.ppermute(block, 'pipe', route)  38.3 us
    ppermute x3, waiting for transfers between devices, share(): return lax.ppermute(block, 'expert', [(i, i ^ 2 * k) for i in range(count)])  25.6 us
    ppermute x3, starting transfers between devices, partner(): return lax.ppermute(block, 'pipe', route)  20.2 us
    all_to_all x1, starting transfers between devices, on_device(): first = lax.all_to_all(first, 'expert', 0, 0, tiled=True).reshape(slots, -1)  18.2 us
    ppermute x3, starting transfers between devices, share(): return lax.ppermute(block, 'expert', [(i, i ^ 2 * k) for i in range(count)])  9.26 us
    all_to_all x1, starting transfers between devices, on_device(): lax.all_to_all(second, 'expert', 0, 0, tiled=True, axis_index_groups=groups)  7.06 us
    pallas_call x1, Pallas kernels, dispatch_shared(): pl.pallas_call(kernel, out_shape=jax.ShapeDtypeStruct(shape, BF), in_spec...  3.06 us
  transfers between devices with their start and end apart: 8, of which 5 were waited for; matrix products, arithmetic and copies ran while one was open for 8% of the time, Pallas kernels for 5%

profile of v4, /device:TPU:1, one launch (start us, length us, event | category | flops | bytes accessed | tf_op | source)
XLA Modules:
  0.0 143.3 jit_solution(17822966054375134310)
XLA Ops:
  0.6 0.0 copy-start
  0.6 2.6 %direct.1 = bf16[64,16,512]{2,1,0:T(8,128)(2,1)} custom-call(s32[8,128]{1,0:T(8,128)} %bitcast.50, f32[8,128]{1,0:T(8,128)} %bitcast.52, bf16[128,1024]{1,0:T(8,128)(2,1)} %bitcast.47), custom_call_target="tpu_custom_call" | custom-call | flops 134217728 | bytes 1048576 | tf_op jit(solution)/shard_map/direct/pallas_call | solution.py:113
  3.2 18.2 %all-to-all-start = ((bf16[64,16,512]{2,1,0:T(8,128)(2,1)}), bf16[64,16,512]{2,1,0:T(8,128)(2,1)S(1)}, u32[]{:S(2)}, u32[]{:S(2)}) async-start(bf16[64,16,512]{2,1,0:T(8,128)(2,1)} %direct.1), calls=%async_computation | async-start | bytes 2097152 | tf_op jit(solution)/shard_map/all_to_all | solution.py:209
  21.5 1.6 %pack.1.refs_1_ = bf16[144,512]{1,0:T(8,128)(2,1)} custom-call(s32[8,128]{1,0:T(8,128)} %bitcast.51, f32[8,128]{1,0:T(8,128)} %bitcast.53, bf16[128,1024]{1,0:T(8,128)(2,1)} %bitcast.48), custom_call_target="tpu_custom_call" | custom-call | flops 65536 | bytes 262144 | tf_op jit(solution)/shard_map/pack/pallas_call | solution.py:65
  23.1 5.1 %collective-permute-start.3 = (bf16[144,512]{1,0:T(8,128)(2,1)}, bf16[144,512]{1,0:T(8,128)(2,1)S(1)}, u32[]{:S(2)}, u32[]{:S(2)}) collective-permute-start(bf16[144,512]{1,0:T(8,128)(2,1)} %pack.1.refs_1_), channel_id=1, source_target_pairs={{0,6},{1,7},{2,4},{3,5},{4,2},{5,3},{6,0},{7,1},{8,14},{9,15},{10,... | collective-permute-start | bytes 442376 | tf_op jit(solution)/shard_map/ppermute | solution.py:171
  28.2 1.9 %collective-permute-start.2 = (bf16[144,512]{1,0:T(8,128)(2,1)}, bf16[144,512]{1,0:T(8,128)(2,1)S(1)}, u32[]{:S(2)}, u32[]{:S(2)}) collective-permute-start(bf16[144,512]{1,0:T(8,128)(2,1)} %pack.1.refs_1_), channel_id=1, source_target_pairs={{0,4},{1,5},{2,6},{3,7},{4,0},{5,1},{6,2},{7,3},{8,12},{9,13},{10,... | collective-permute-start | bytes 442376 | tf_op jit(solution)/shard_map/ppermute | solution.py:171
  30.1 2.3 %collective-permute-start.1 = (bf16[144,512]{1,0:T(8,128)(2,1)}, bf16[144,512]{1,0:T(8,128)(2,1)S(1)}, u32[]{:S(2)}, u32[]{:S(2)}) collective-permute-start(bf16[144,512]{1,0:T(8,128)(2,1)} %pack.1.refs_1_), channel_id=1, source_target_pairs={{0,2},{1,3},{2,0},{3,1},{4,6},{5,7},{6,4},{7,5},{8,10},{9,11},{10,... | collective-permute-start | bytes 442376 | tf_op jit(solution)/shard_map/ppermute | solution.py:171
  32.4 0.0 copy-done
  32.4 1.0 dynamic-slice_bitcast_fusion
  33.4 0.1 copy.9
  33.5 1.1 constant_dynamic-slice_fusion
  34.6 15.8 %collective-permute-done.3.refs_4_ = bf16[144,512]{1,0:T(8,128)(2,1)S(1)} collective-permute-done((bf16[144,512]{1,0:T(8,128)(2,1)}, bf16[144,512]{1,0:T(8,128)(2,1)S(1)}, u32[]{:S(2)}, u32[]{:S(2)}) %collective-permute-start.3) | collective-permute-done | bytes 147488 | tf_op jit(solution)/shard_map/ppermute | solution.py:171
  50.4 0.0 copy-start.3
  50.4 9.7 %collective-permute-done.2.refs_3_ = bf16[144,512]{1,0:T(8,128)(2,1)S(1)} collective-permute-done((bf16[144,512]{1,0:T(8,128)(2,1)}, bf16[144,512]{1,0:T(8,128)(2,1)S(1)}, u32[]{:S(2)}, u32[]{:S(2)}) %collective-permute-start.2) | collective-permute-done | bytes 147488 | tf_op jit(solution)/shard_map/ppermute | solution.py:171
  60.1 0.0 copy-start.4
  60.1 0.0 collective-permute-done.1.refs_2_
  60.1 0.0 copy-start.5
  60.2 0.0 copy-done.3
  60.2 0.6 copy-done.4
  60.8 0.1 copy-done.5
  60.9 3.1 %shared.1 = bf16[16,4,16,512]{3,2,1,0:T(8,128)(2,1)} custom-call(s32[1]{0:T(128)} %bitcast.8.refs_0_, bf16[144,512]{1,0:T(8,128)(2,1)} %pack.1.refs_1_, bf16[144,512]{1,0:T(8,128)(2,1)} %copy-done.5, bf16[144,512]{1,0:T(8,128)(2,1)} %copy-done.4, bf16[144,512]{1,0:T(8,128)(2,1)} %copy-done.3), custom_call_target="tpu_custom_call" | custom-call | flops 134217728 | bytes 1048576 | tf_op jit(solution)/shard_map/shared/pallas_call | solution.py:153
  63.9 0.0 all-to-all-done
  63.9 7.1 %all-to-all-start.1 = ((bf16[16,4,16,512]{3,2,1,0:T(8,128)(2,1)}), bf16[16,4,16,512]{3,2,1,0:T(8,128)(2,1)S(1)}, u32[]{:S(2)}, u32[]{:S(2)}) async-start(bf16[16,4,16,512]{3,2,1,0:T(8,128)(2,1)} %shared.1), calls=%async_computation.1 | async-start | bytes 2097152 | tf_op jit(solution)/shard_map/all_to_all | solution.py:212
  71.0 2.1 %dequant.1 = bf16[1024,256]{1,0:T(8,128)(2,1)} custom-call(f32[2,8]{1,0:T(2,128)} %bitcast.54, bf16[256,1024]{1,0:T(8,128)(2,1)} %bitcast.49), custom_call_target="tpu_custom_call" | custom-call | flops 262144 | bytes 1048576 | tf_op jit(solution)/shard_map/dequant/pallas_call | solution.py:31
  73.0 11.0 %collective-permute-start = (bf16[1024,256]{1,0:T(8,128)(2,1)}, bf16[1024,256]{1,0:T(8,128)(2,1)}, u32[]{:S(2)}, u32[]{:S(2)}) collective-permute-start(bf16[1024,256]{1,0:T(8,128)(2,1)} %dequant.1), channel_id=1, source_target_pairs={{0,512},{64,576},{128,640},{192,704},{256,768},{320,832},{384,896}... | collective-permute-start | bytes 1572872 | tf_op jit(solution)/shard_map/ppermute | solution.py:166
  84.1 23.8 %collective-permute-done = bf16[1024,256]{1,0:T(8,128)(2,1)} collective-permute-done((bf16[1024,256]{1,0:T(8,128)(2,1)}, bf16[1024,256]{1,0:T(8,128)(2,1)}, u32[]{:S(2)}, u32[]{:S(2)}) %collective-permute-start) | collective-permute-done | bytes 524320 | tf_op jit(solution)/shard_map/ppermute | solution.py:166
  107.9 1.8 %maximum_select_fusion = bf16[1024,512]{1,0:T(8,128)(2,1)S(1)} fusion(bf16[1024,256]{1,0:T(8,128)(2,1)} %dequant.1, bf16[1024,256]{1,0:T(8,128)(2,1)} %collective-permute-done, pred[]{:T(512)S(6)} %eq.5), kind=kLoop, calls=%fused_computation.6 | loop fusion | flops 4718592 | bytes 2097153 | tf_op jit(solution)/shard_map/jit(_where)/select_n | solution.py:222
  109.7 1.5 %convolution_convert_fusion.3 = bf16[256,512]{1,0:T(8,128)(2,1)S(1)} fusion(bf16[1024,256]{1,0:T(8,128)(2,1)} %get-tuple-element.8, bf16[1024,512]{1,0:T(8,128)(2,1)S(1)} %bitcast.44), kind=kOutput, calls=%fused_computation.5 | convolution fusion | flops 268566528 | bytes 1835008 | tf_op jit(solution)/shard_map/dot_general | solution.py:220
  111.2 2.2 %convolution_convert_fusion.2 = bf16[256,512]{1,0:T(8,128)(2,1)} fusion(bf16[1024,256]{1,0:T(8,128)(2,1)} %get-tuple-element.9, bf16[1024,512]{1,0:T(8,128)(2,1)S(1)} %bitcast.45), kind=kOutput, calls=%fused_computation.4 | convolution fusion | flops 268566528 | bytes 1835008 | tf_op jit(solution)/shard_map/dot_general | solution.py:218
  113.4 4.2 %collective-permute-start.4 = (bf16[256,512]{1,0:T(8,128)(2,1)}, bf16[256,512]{1,0:T(8,128)(2,1)}, u32[]{:S(2)}, u32[]{:S(2)}) collective-permute-start(bf16[256,512]{1,0:T(8,128)(2,1)} %convolution_convert_fusion.2), channel_id=1, source_target_pairs={{0,512},{64,576},{128,640},{192,704},{256,768},{320,832},{384,896}... | collective-permute-start | bytes 786440 | tf_op jit(solution)/shard_map/ppermute | solution.py:166
  117.6 0.0 all-to-all-done.1
  117.6 0.0 copy-start.2
  117.6 0.1 copy.10
  117.7 0.9 copy-done.2
  118.7 0.5 convolution_convert_fusion
  119.1 5.0 %collective-permute-start.5 = (bf16[256,512]{1,0:T(8,128)(2,1)S(1)}, bf16[256,512]{1,0:T(8,128)(2,1)S(1)}, u32[]{:S(2)}, u32[]{:S(2)}) collective-permute-start(bf16[256,512]{1,0:T(8,128)(2,1)S(1)} %convolution_convert_fusion), channel_id=1, source_target_pairs={{0,512},{64,576},{128,640},{192,704},{256,768},{320,832},{384,896}... | collective-permute-start | bytes 786440 | tf_op jit(solution)/shard_map/ppermute | solution.py:166
  124.1 0.7 fusion.1
  124.8 0.0 copy-start.1
  124.8 1.7 %fusion = bf16[1,1,1,1024,512]{4,3,2,1,0:T(8,128)(2,1)} fusion(f32[1024,512]{1,0:T(8,128)S(1)} %fusion.1, bf16[1024,512]{1,0:T(8,128)(2,1)S(1)} %bitcast.46, bf16[1024,512]{1,0:T(8,128)(2,1)S(1)} %maximum_select_fusion), kind=kOutput, calls=%fused_computation.1 | convolution fusion | flops 537919488 | bytes 4718592 | tf_op jit(solution)/shard_map/dot_general | solution.py:230
  126.5 0.0 copy-done.1
  126.5 0.5 convolution_convert_fusion.1
  127.0 9.5 %collective-permute-done.4 = bf16[256,512]{1,0:T(8,128)(2,1)} collective-permute-done((bf16[256,512]{1,0:T(8,128)(2,1)}, bf16[256,512]{1,0:T(8,128)(2,1)}, u32[]{:S(2)}, u32[]{:S(2)}) %collective-permute-start.4) | collective-permute-done | bytes 262176 | tf_op jit(solution)/shard_map/ppermute | solution.py:166
  136.4 1.0 add_convert_fusion.2
  137.5 4.9 %collective-permute-done.5 = bf16[256,512]{1,0:T(8,128)(2,1)S(1)} collective-permute-done((bf16[256,512]{1,0:T(8,128)(2,1)S(1)}, bf16[256,512]{1,0:T(8,128)(2,1)S(1)}, u32[]{:S(2)}, u32[]{:S(2)}) %collective-permute-start.5) | collective-permute-done | bytes 262176 | tf_op jit(solution)/shard_map/ppermute | solution.py:166
  142.4 0.1 add_convert_fusion.1
  142.5 0.9 maximum_bitcast_fusion
Async XLA Ops:
  0.6 31.7 %copy-start = (bf16[1,1,1,1024,512]{4,3,2,1,0:T(8,128)(2,1)S(1)}, bf16[1,1,1,1024,512]{4,3,2,1,0:T(8,128)(2,1)}, u32[]{:S(2)}) copy-start(bf16[1,1,1,1024,512]{4,3,2,1,0:T(8,128)(2,1)} %param.9) | copy-start | bytes 3145732
  3.2 60.7 %all-to-all-start = ((bf16[64,16,512]{2,1,0:T(8,128)(2,1)}), bf16[64,16,512]{2,1,0:T(8,128)(2,1)S(1)}, u32[]{:S(2)}, u32[]{:S(2)}) async-start(bf16[64,16,512]{2,1,0:T(8,128)(2,1)} %direct.1), calls=%async_computation | async-start | bytes 2097152 | tf_op jit(solution)/shard_map/all_to_all | solution.py:209
  23.1 27.4 %collective-permute-start.3 = (bf16[144,512]{1,0:T(8,128)(2,1)}, bf16[144,512]{1,0:T(8,128)(2,1)S(1)}, u32[]{:S(2)}, u32[]{:S(2)}) collective-permute-start(bf16[144,512]{1,0:T(8,128)(2,1)} %pack.1.refs_1_), channel_id=1, source_target_pairs={{0,6},{1,7},{2,4},{3,5},{4,2},{5,3},{6,0},{7,1},{8,14},{9,15},{10,... | collective-permute-start | bytes 442376 | tf_op jit(solution)/shard_map/ppermute | solution.py:171
  28.2 32.0 %collective-permute-start.2 = (bf16[144,512]{1,0:T(8,128)(2,1)}, bf16[144,512]{1,0:T(8,128)(2,1)S(1)}, u32[]{:S(2)}, u32[]{:S(2)}) collective-permute-start(bf16[144,512]{1,0:T(8,128)(2,1)} %pack.1.refs_1_), channel_id=1, source_target_pairs={{0,4},{1,5},{2,6},{3,7},{4,0},{5,1},{6,2},{7,3},{8,12},{9,13},{10,... | collective-permute-start | bytes 442376 | tf_op jit(solution)/shard_map/ppermute | solution.py:171
  30.1 30.1 %collective-permute-start.1 = (bf16[144,512]{1,0:T(8,128)(2,1)}, bf16[144,512]{1,0:T(8,128)(2,1)S(1)}, u32[]{:S(2)}, u32[]{:S(2)}) collective-permute-start(bf16[144,512]{1,0:T(8,128)(2,1)} %pack.1.refs_1_), channel_id=1, source_target_pairs={{0,2},{1,3},{2,0},{3,1},{4,6},{5,7},{6,4},{7,5},{8,10},{9,11},{10,... | collective-permute-start | bytes 442376 | tf_op jit(solution)/shard_map/ppermute | solution.py:171
  50.4 9.7 %copy-start.3 = (bf16[144,512]{1,0:T(8,128)(2,1)}, bf16[144,512]{1,0:T(8,128)(2,1)S(1)}, u32[]{:S(2)}) copy-start(bf16[144,512]{1,0:T(8,128)(2,1)S(1)} %collective-permute-done.3.refs_4_) | copy-start | bytes 442372
  60.1 0.7 copy-start.4
  60.1 0.7 copy-start.5
  63.9 53.7 %all-to-all-start.1 = ((bf16[16,4,16,512]{3,2,1,0:T(8,128)(2,1)}), bf16[16,4,16,512]{3,2,1,0:T(8,128)(2,1)S(1)}, u32[]{:S(2)}, u32[]{:S(2)}) async-start(bf16[16,4,16,512]{3,2,1,0:T(8,128)(2,1)} %shared.1), calls=%async_computation.1 | async-start | bytes 2097152 | tf_op jit(solution)/shard_map/all_to_all | solution.py:212
  73.0 34.9 %collective-permute-start = (bf16[1024,256]{1,0:T(8,128)(2,1)}, bf16[1024,256]{1,0:T(8,128)(2,1)}, u32[]{:S(2)}, u32[]{:S(2)}) collective-permute-start(bf16[1024,256]{1,0:T(8,128)(2,1)} %dequant.1), channel_id=1, source_target_pairs={{0,512},{64,576},{128,640},{192,704},{256,768},{320,832},{384,896}... | collective-permute-start | bytes 1572872 | tf_op jit(solution)/shard_map/ppermute | solution.py:166
  113.4 23.0 %collective-permute-start.4 = (bf16[256,512]{1,0:T(8,128)(2,1)}, bf16[256,512]{1,0:T(8,128)(2,1)}, u32[]{:S(2)}, u32[]{:S(2)}) collective-permute-start(bf16[256,512]{1,0:T(8,128)(2,1)} %convolution_convert_fusion.2), channel_id=1, source_target_pairs={{0,512},{64,576},{128,640},{192,704},{256,768},{320,832},{384,896}... | collective-permute-start | bytes 786440 | tf_op jit(solution)/shard_map/ppermute | solution.py:166
  117.6 1.0 copy-start.2
  119.1 23.3 %collective-permute-start.5 = (bf16[256,512]{1,0:T(8,128)(2,1)S(1)}, bf16[256,512]{1,0:T(8,128)(2,1)S(1)}, u32[]{:S(2)}, u32[]{:S(2)}) collective-permute-start(bf16[256,512]{1,0:T(8,128)(2,1)S(1)} %convolution_convert_fusion), channel_id=1, source_target_pairs={{0,512},{64,576},{128,640},{192,704},{256,768},{320,832},{384,896}... | collective-permute-start | bytes 786440 | tf_op jit(solution)/shard_map/ppermute | solution.py:166
  124.8 1.7 %copy-start.1 = (bf16[1024,256]{1,0:T(8,128)(2,1)S(1)}, bf16[1024,256]{1,0:T(8,128)(2,1)}, u32[]{:S(2)}) copy-start(bf16[1024,256]{1,0:T(8,128)(2,1)} %get-tuple-element.10) | copy-start | bytes 1572868

commit v5 on v4

--- a/solution.py
+++ b/solution.py
@@ -13,29 +13,34 @@
 VM = pl.BlockSpec(memory_space=pltpu.VMEM)
 SM = pl.BlockSpec(memory_space=pltpu.SMEM)
 
+PARAMS = pltpu.CompilerParams(vmem_limit_bytes=16 << 20)
+
 
 def cost(flops, nbytes):
     return pl.CostEstimate(flops=flops, bytes_accessed=nbytes, transcendentals=0)
 
 
-def dequant_kernel(scale_ref, weight_ref, out_ref):
-    rows, cols = weight_ref.shape
-    for i in range(rows // QBLOCK):
-        for j in range(cols // QBLOCK):
-            here, there = pl.ds(i * QBLOCK, QBLOCK), pl.ds(j * QBLOCK, QBLOCK)
-            block = weight_ref[here, there].astype(F32) * scale_ref[i, j]
-            out_ref[there, here] = block.T.astype(BF)
-
-
-def dequantize(weight, scales):
+def dequant_kernel(scale_ref, *refs):
+    weight_refs, out_ref = refs[:-1], refs[-1]
+    blocks = [(r, i) for r in weight_refs for i in range(r.shape[0] // QBLOCK)]
+    for at, (ref, i) in enumerate(blocks):
+        for j in range(ref.shape[1] // QBLOCK):
+            there = pl.ds(j * QBLOCK, QBLOCK)
+            block = ref[pl.ds(i * QBLOCK, QBLOCK), there].astype(F32) * scale_ref[at, j]
+            out_ref[there, pl.ds(at * QBLOCK, QBLOCK)] = block.T.astype(BF)
+
+
+def dequantize(scales, *weights):
+    rows, cols = sum(w.shape[0] for w in weights), weights[0].shape[1]
     return pl.pallas_call(
         dequant_kernel,
-        out_shape=jax.ShapeDtypeStruct(weight.shape[::-1], BF),
-        in_specs=[SM, VM],
+        out_shape=jax.ShapeDtypeStruct((cols, rows), BF),
+        in_specs=[SM] + [VM] * len(weights),
         out_specs=VM,
         name="dequant",
-        cost_estimate=cost(weight.size, weight.size * 4),
-    )(scales, weight)
+        compiler_params=PARAMS,
+        cost_estimate=cost(rows * cols, rows * cols * 4),
+    )(scales, *weights)
 
 
 def pack_kernel(route_ref, gate_ref, grad_ref, out_ref):
@@ -156,6 +161,7 @@
         in_specs=[SM] + [VM] * len(blocks),
         out_specs=VM,
         name="shared",
+        compiler_params=PARAMS,
         cost_estimate=cost(2 * size * toks, size * 2),
     )(side, *blocks)
 
@@ -187,12 +193,16 @@
     ]
     routes, gates = routes[0, 0].T, gate_weights[0, 0].T
 
+    weight, scales = down_weight[0, 0], block_scales[0, 0]
+    cut = weight.shape[0] // 2
+    other_top = partner(weight[:cut])
     packed = pack(routes, gates, grad)
-    blocks = [packed]
-    for k in range(1, RUN):
-        blocks.append(share(packed, k))
-    own_half = dequantize(down_weight[0, 0], block_scales[0, 0])
-    other_half = partner(own_half)
+    far = share(packed, 2)
+    near = share(packed, 1)
+    corner = share(far, 1)
+    blocks = [packed, near, far, corner]
+    other_low = partner(weight[cut:])
+    other_scales = partner(scales)
 
     act = hidden_act[0, 0, 0]
     ff = act.shape[1]
@@ -219,6 +229,8 @@
         sent.append(partner(part))
         part = lax.dot_general(keep, rows, ROWS_ROWS, preferred_element_type=F32)
         kept.append(lax.optimization_barrier(part.astype(BF)))
+    own_half = dequantize(scales, weight)
+    other_half = dequantize(other_scales, other_top, other_low)
     whole = jnp.where(
         upper == 1,
         jnp.concatenate([other_half, own_half], axis=1),

time: 144 us -> 138 us (0.958)
  the two profiles are of different devices: /device:TPU:1 before, /device:TPU:4 now
where the time goes in v5:
time: 138 us; the launch traced here: 137 us
  starting transfers between devices  67.1 us (49%)
  waiting for transfers between devices  47.9 us (35%)
  Pallas kernels  7.64 us (6%)
  matrix products  7.36 us (5%)
  local copies, waits for them, and re-layouts  3.95 us (3%)
  other arithmetic  2.25 us (2%)
    ppermute x5, starting transfers between devices, partner(): return lax.ppermute(block, 'pipe', route)  34.2 us
    ppermute x3, waiting for transfers between devices, share(): return lax.ppermute(block, 'expert', [(i, i ^ 2 * k) for i in range(count)])  26.5 us
    ppermute x5, waiting for transfers between devices, partner(): return lax.ppermute(block, 'pipe', route)  21.4 us
    all_to_all x1, starting transfers between devices, on_device(): first = lax.all_to_all(first, 'expert', 0, 0, tiled=True).reshape(slots, -1)  16.7 us
    ppermute x3, starting transfers between devices, share(): return lax.ppermute(block, 'expert', [(i, i ^ 2 * k) for i in range(count)])  9.65 us
    all_to_all x1, starting transfers between devices, on_device(): lax.all_to_all(second, 'expert', 0, 0, tiled=True, axis_index_groups=groups)  6.52 us
    dot_general x2, matrix products, on_device(): lax.dot_general(send, rows, ROWS_ROWS, preferred_element_type=F32)  2.85 us
  transfers between devices with their start and end apart: 10, of which 5 were waited for; matrix products, arithmetic and copies ran while one was open for 9% of the time, Pallas kernels for 4%

profile of v5, /device:TPU:4, one launch (start us, length us, event | category | flops | bytes accessed | tf_op | source)
XLA Modules:
  0.0 137.1 jit_solution(2226323071549419362)
XLA Ops:
  0.6 0.0 copy-start.5
  0.6 2.6 %direct.1 = bf16[64,16,512]{2,1,0:T(8,128)(2,1)} custom-call(s32[8,128]{1,0:T(8,128)} %bitcast.53, f32[8,128]{1,0:T(8,128)} %bitcast.55, bf16[128,1024]{1,0:T(8,128)(2,1)} %bitcast.51), custom_call_target="tpu_custom_call" | custom-call | flops 134217728 | bytes 1048576 | tf_op jit(solution)/shard_map/direct/pallas_call | solution.py:118
  3.2 16.7 %all-to-all-start = ((bf16[64,16,512]{2,1,0:T(8,128)(2,1)}), bf16[64,16,512]{2,1,0:T(8,128)(2,1)S(1)}, u32[]{:S(2)}, u32[]{:S(2)}) async-start(bf16[64,16,512]{2,1,0:T(8,128)(2,1)} %direct.1), calls=%async_computation | async-start | bytes 2097152 | tf_op jit(solution)/shard_map/all_to_all | solution.py:219
  20.0 1.6 %pack.1.refs_1_ = bf16[144,512]{1,0:T(8,128)(2,1)} custom-call(s32[8,128]{1,0:T(8,128)} %bitcast.54, f32[8,128]{1,0:T(8,128)} %bitcast.56, bf16[128,1024]{1,0:T(8,128)(2,1)} %bitcast.52), custom_call_target="tpu_custom_call" | custom-call | flops 65536 | bytes 262144 | tf_op jit(solution)/shard_map/pack/pallas_call | solution.py:70
  21.6 4.4 %collective-permute-start.4 = (bf16[144,512]{1,0:T(8,128)(2,1)}, bf16[144,512]{1,0:T(8,128)(2,1)S(1)}, u32[]{:S(2)}, u32[]{:S(2)}) collective-permute-start(bf16[144,512]{1,0:T(8,128)(2,1)} %pack.1.refs_1_), channel_id=1, source_target_pairs={{0,4},{1,5},{2,6},{3,7},{4,0},{5,1},{6,2},{7,3},{8,12},{9,13},{10,... | collective-permute-start | bytes 442376 | tf_op jit(solution)/shard_map/ppermute | solution.py:177
  25.9 3.4 %collective-permute-start.3 = (bf16[144,512]{1,0:T(8,128)(2,1)}, bf16[144,512]{1,0:T(8,128)(2,1)S(1)}, u32[]{:S(2)}, u32[]{:S(2)}) collective-permute-start(bf16[144,512]{1,0:T(8,128)(2,1)} %pack.1.refs_1_), channel_id=1, source_target_pairs={{0,2},{1,3},{2,0},{3,1},{4,6},{5,7},{6,4},{7,5},{8,10},{9,11},{10,... | collective-permute-start | bytes 442376 | tf_op jit(solution)/shard_map/ppermute | solution.py:177
  29.3 23.0 %collective-permute-done.4.refs_3_ = bf16[144,512]{1,0:T(8,128)(2,1)S(1)} collective-permute-done((bf16[144,512]{1,0:T(8,128)(2,1)}, bf16[144,512]{1,0:T(8,128)(2,1)S(1)}, u32[]{:S(2)}, u32[]{:S(2)}) %collective-permute-start.4) | collective-permute-done | bytes 147488 | tf_op jit(solution)/shard_map/ppermute | solution.py:177
  52.3 1.9 %collective-permute-start.5 = (bf16[144,512]{1,0:T(8,128)(2,1)S(1)}, bf16[144,512]{1,0:T(8,128)(2,1)S(1)}, u32[]{:S(2)}, u32[]{:S(2)}) collective-permute-start(bf16[144,512]{1,0:T(8,128)(2,1)S(1)} %collective-permute-done.4.refs_3_), channel_id=1, source_target_pairs={{0,2},{1,3},{2,0},{3,1},{4,6},{5,7},{6,4},{7,5},{8,10},{9,11},{10,... | collective-permute-start | bytes 442376 | tf_op jit(solution)/shard_map/ppermute | solution.py:177
  54.2 0.0 copy-done.5
  54.2 1.1 dynamic-slice_bitcast_fusion
  55.3 0.0 copy-start.1
  55.3 0.1 copy.9
  55.4 1.1 constant_dynamic-slice_fusion
  56.4 0.0 copy-start
  56.4 0.0 collective-permute-done.3.refs_2_
  56.4 3.5 %collective-permute-done.5.refs_4_ = bf16[144,512]{1,0:T(8,128)(2,1)S(1)} collective-permute-done((bf16[144,512]{1,0:T(8,128)(2,1)S(1)}, bf16[144,512]{1,0:T(8,128)(2,1)S(1)}, u32[]{:S(2)}, u32[]{:S(2)}) %collective-permute-start.5) | collective-permute-done | bytes 147488 | tf_op jit(solution)/shard_map/ppermute | solution.py:177
  59.9 0.0 copy-done.1
  59.9 0.0 copy-start.2
  59.9 1.9 %shared.1 = bf16[16,4,16,512]{3,2,1,0:T(8,128)(2,1)} custom-call(s32[1]{0:T(128)} %bitcast.10.refs_0_, bf16[144,512]{1,0:T(8,128)(2,1)S(1)} %copy-done.1, bf16[144,512]{1,0:T(8,128)(2,1)S(1)} %collective-permute-done.3.refs_2_, bf16[144,512]{1,0:T(8,128)(2,1)S(1)} %collective-permute-done.4.refs_3_, bf16[144,512]{1,0:T(8,128)(2,1)S(1)} %collective-permute-done.5.refs_4_), custom_call_target="tpu_custom_call" | custom-call | flops 134217728 | bytes 1048576 | tf_op jit(solution)/shard_map/shared/pallas_call | solution.py:158
  61.8 0.0 all-to-all-done
  61.9 0.0 copy-start.3
  61.9 6.5 %all-to-all-start.1 = ((bf16[16,4,16,512]{3,2,1,0:T(8,128)(2,1)}), bf16[16,4,16,512]{3,2,1,0:T(8,128)(2,1)}, u32[]{:S(2)}, u32[]{:S(2)}) async-start(bf16[16,4,16,512]{3,2,1,0:T(8,128)(2,1)} %shared.1), calls=%async_computation.1 | async-start | bytes 2097152 | tf_op jit(solution)/shard_map/all_to_all | solution.py:222
  68.4 0.0 copy-done
  68.4 11.8 %collective-permute-start.2 = (bf16[128,1024]{1,0:T(8,128)(2,1)S(1)}, bf16[128,1024]{1,0:T(8,128)(2,1)S(1)}, u32[]{:S(2)}, u32[]{:S(2)}) collective-permute-start(bf16[128,1024]{1,0:T(8,128)(2,1)S(1)} %get-tuple-element.16), channel_id=1, source_target_pairs={{0,512},{64,576},{128,640},{192,704},{256,768},{320,832},{384,896}... | collective-permute-start | bytes 786440 | tf_op jit(solution)/shard_map/ppermute | solution.py:172
  80.3 1.9 %collective-permute-start.1 = (bf16[128,1024]{1,0:T(8,128)(2,1)S(1)}, bf16[128,1024]{1,0:T(8,128)(2,1)S(1)}, u32[]{:S(2)}, u32[]{:S(2)}) collective-permute-start(bf16[128,1024]{1,0:T(8,128)(2,1)S(1)} %get-tuple-element.17), channel_id=1, source_target_pairs={{0,512},{64,576},{128,640},{192,704},{256,768},{320,832},{384,896}... | collective-permute-start | bytes 786440 | tf_op jit(solution)/shard_map/ppermute | solution.py:172
  82.2 0.0 copy-done.2
  82.2 7.8 %collective-permute-start = (f32[2,8]{1,0:T(2,128)S(1)}, f32[2,8]{1,0:T(2,128)S(1)}, u32[]{:S(2)}, u32[]{:S(2)}) collective-permute-start(f32[2,8]{1,0:T(2,128)S(1)} %bitcast.43), channel_id=1, source_target_pairs={{0,512},{64,576},{128,640},{192,704},{256,768},{320,832},{384,896}... | collective-permute-start | bytes 200 | tf_op jit(solution)/shard_map/ppermute | solution.py:172
  90.1 0.0 copy-start.7
  90.1 0.8 dequant.3
  90.9 0.0 copy-done.3
  90.9 8.3 %collective-permute-done.scale_ref = f32[2,8]{1,0:T(2,128)S(1)} collective-permute-done((f32[2,8]{1,0:T(2,128)S(1)}, f32[2,8]{1,0:T(2,128)S(1)}, u32[]{:S(2)}, u32[]{:S(2)}) %collective-permute-start) | collective-permute-done | bytes 96 | tf_op jit(solution)/shard_map/ppermute | solution.py:172
  99.1 0.0 copy-start.4
  99.1 0.0 collective-permute-done.2.refs_1_
  99.1 0.0 collective-permute-done.1.refs_0_
  99.1 0.8 dequant.2
  99.9 0.0 copy-start.6
  99.9 0.3 maximum_select_fusion
  100.2 0.0 copy-done.7
  100.2 0.1 copy-done.4
  100.3 0.5 convolution_convert_fusion.3
  100.8 0.2 copy-done.6
  101.0 1.2 convolution_convert_fusion.2
  102.2 10.7 %collective-permute-start.6 = (bf16[256,512]{1,0:T(8,128)(2,1)}, bf16[256,512]{1,0:T(8,128)(2,1)}, u32[]{:S(2)}, u32[]{:S(2)}) collective-permute-start(bf16[256,512]{1,0:T(8,128)(2,1)} %convolution_convert_fusion.2), channel_id=1, source_target_pairs={{0,512},{64,576},{128,640},{192,704},{256,768},{320,832},{384,896}... | collective-permute-start | bytes 786440 | tf_op jit(solution)/shard_map/ppermute | solution.py:172
  112.9 0.7 fusion.2
  113.6 0.0 all-to-all-done.1
  113.6 0.0 copy-start.9
  113.6 1.4 copy.10
  115.0 0.0 copy-done.9
  115.0 1.7 %convolution_convert_fusion = bf16[256,512]{1,0:T(8,128)(2,1)S(1)} fusion(bf16[1024,256]{1,0:T(8,128)(2,1)S(1)} %copy-done.9, bf16[1024,512]{1,0:T(8,128)(2,1)} %bitcast.22), kind=kOutput, calls=%fused_computation.2 | convolution fusion | flops 268566528 | bytes 1835008 | tf_op jit(solution)/shard_map/dot_general | solution.py:228
  116.7 1.9 %collective-permute-start.7 = (bf16[256,512]{1,0:T(8,128)(2,1)S(1)}, bf16[256,512]{1,0:T(8,128)(2,1)S(1)}, u32[]{:S(2)}, u32[]{:S(2)}) collective-permute-start(bf16[256,512]{1,0:T(8,128)(2,1)S(1)} %convolution_convert_fusion), channel_id=1, source_target_pairs={{0,512},{64,576},{128,640},{192,704},{256,768},{320,832},{384,896}... | collective-permute-start | bytes 786440 | tf_op jit(solution)/shard_map/ppermute | solution.py:172
  118.6 0.0 copy-start.8
  118.6 1.7 %fusion = bf16[1,1,1,1024,512]{4,3,2,1,0:T(8,128)(2,1)} fusion(f32[1024,512]{1,0:T(8,128)S(1)} %fusion.2, bf16[1024,512]{1,0:T(8,128)(2,1)S(1)} %bitcast.50, bf16[1024,512]{1,0:T(8,128)(2,1)S(1)} %maximum_select_fusion), kind=kOutput, calls=%fused_computation.1 | convolution fusion | flops 537919488 | bytes 4718592 | tf_op jit(solution)/shard_map/dot_general | solution.py:243
  120.3 0.0 copy-done.8
  120.3 1.7 %convolution_convert_fusion.1 = bf16[256,512]{1,0:T(8,128)(2,1)S(1)} fusion(bf16[1024,256]{1,0:T(8,128)(2,1)S(1)} %copy-done.8, bf16[1024,512]{1,0:T(8,128)(2,1)} %bitcast.22), kind=kOutput, calls=%fused_computation.3 | convolution fusion | flops 268566528 | bytes 1835008 | tf_op jit(solution)/shard_map/dot_general | solution.py:230
  122.0 3.9 %collective-permute-done.6 = bf16[256,512]{1,0:T(8,128)(2,1)} collective-permute-done((bf16[256,512]{1,0:T(8,128)(2,1)}, bf16[256,512]{1,0:T(8,128)(2,1)}, u32[]{:S(2)}, u32[]{:S(2)}) %collective-permute-start.6) | collective-permute-done | bytes 262176 | tf_op jit(solution)/shard_map/ppermute | solution.py:172
  125.9 1.0 add_convert_fusion.2
  126.9 9.2 %collective-permute-done.7 = bf16[256,512]{1,0:T(8,128)(2,1)S(1)} collective-permute-done((bf16[256,512]{1,0:T(8,128)(2,1)S(1)}, bf16[256,512]{1,0:T(8,128)(2,1)S(1)}, u32[]{:S(2)}, u32[]{:S(2)}) %collective-permute-start.7) | collective-permute-done | bytes 262176 | tf_op jit(solution)/shard_map/ppermute | solution.py:172
  136.2 0.1 add_convert_fusion.1
  136.2 0.9 maximum_bitcast_fusion
  (1 shorter events, 0.0 us)
Async XLA Ops:
  0.6 53.6 %copy-start.5 = (bf16[1,1,1,1024,512]{4,3,2,1,0:T(8,128)(2,1)S(1)}, bf16[1,1,1,1024,512]{4,3,2,1,0:T(8,128)(2,1)}, u32[]{:S(2)}) copy-start(bf16[1,1,1,1024,512]{4,3,2,1,0:T(8,128)(2,1)} %param.9) | copy-start | bytes 3145732
  3.2 58.6 %all-to-all-start = ((bf16[64,16,512]{2,1,0:T(8,128)(2,1)}), bf16[64,16,512]{2,1,0:T(8,128)(2,1)S(1)}, u32[]{:S(2)}, u32[]{:S(2)}) async-start(bf16[64,16,512]{2,1,0:T(8,128)(2,1)} %direct.1), calls=%async_computation | async-start | bytes 2097152 | tf_op jit(solution)/shard_map/all_to_all | solution.py:219
  21.6 30.7 %collective-permute-start.4 = (bf16[144,512]{1,0:T(8,128)(2,1)}, bf16[144,512]{1,0:T(8,128)(2,1)S(1)}, u32[]{:S(2)}, u32[]{:S(2)}) collective-permute-start(bf16[144,512]{1,0:T(8,128)(2,1)} %pack.1.refs_1_), channel_id=1, source_target_pairs={{0,4},{1,5},{2,6},{3,7},{4,0},{5,1},{6,2},{7,3},{8,12},{9,13},{10,... | collective-permute-start | bytes 442376 | tf_op jit(solution)/shard_map/ppermute | solution.py:177
  25.9 30.5 %collective-permute-start.3 = (bf16[144,512]{1,0:T(8,128)(2,1)}, bf16[144,512]{1,0:T(8,128)(2,1)S(1)}, u32[]{:S(2)}, u32[]{:S(2)}) collective-permute-start(bf16[144,512]{1,0:T(8,128)(2,1)} %pack.1.refs_1_), channel_id=1, source_target_pairs={{0,2},{1,3},{2,0},{3,1},{4,6},{5,7},{6,4},{7,5},{8,10},{9,11},{10,... | collective-permute-start | bytes 442376 | tf_op jit(solution)/shard_map/ppermute | solution.py:177
  52.3 7.6 %collective-permute-start.5 = (bf16[144,512]{1,0:T(8,128)(2,1)S(1)}, bf16[144,512]{1,0:T(8,128)(2,1)S(1)}, u32[]{:S(2)}, u32[]{:S(2)}) collective-permute-start(bf16[144,512]{1,0:T(8,128)(2,1)S(1)} %collective-permute-done.4.refs_3_), channel_id=1, source_target_pairs={{0,2},{1,3},{2,0},{3,1},{4,6},{5,7},{6,4},{7,5},{8,10},{9,11},{10,... | collective-permute-start | bytes 442376 | tf_op jit(solution)/shard_map/ppermute | solution.py:177
  55.3 4.6 %copy-start.1 = (bf16[144,512]{1,0:T(8,128)(2,1)S(1)}, bf16[144,512]{1,0:T(8,128)(2,1)}, u32[]{:S(2)}) copy-start(bf16[144,512]{1,0:T(8,128)(2,1)} %pack.1.refs_1_) | copy-start | bytes 442372
  56.4 12.0 %copy-start = (bf16[1,1,256,1024]{3,2,1,0:T(8,128)(2,1)S(1)}, bf16[1,1,256,1024]{3,2,1,0:T(8,128)(2,1)}, u32[]{:S(2)}) copy-start(bf16[1,1,256,1024]{3,2,1,0:T(8,128)(2,1)} %param.10) | copy-start | bytes 1572868
  59.9 22.3 %copy-start.2 = (f32[1,1,2,8]{3,2,1,0:T(2,128)S(1)}, f32[1,1,2,8]{3,2,1,0:T(2,128)}, u32[]{:S(2)}) copy-start(f32[1,1,2,8]{3,2,1,0:T(2,128)} %param.11) | copy-start | bytes 196
  61.9 29.0 %copy-start.3 = (bf16[64,16,512]{2,1,0:T(8,128)(2,1)}, bf16[64,16,512]{2,1,0:T(8,128)(2,1)S(1)}, u32[]{:S(2)}) copy-start(bf16[64,16,512]{2,1,0:T(8,128)(2,1)S(1)} %all-to-all-done) | copy-start | bytes 3145732
  61.9 51.7 %all-to-all-start.1 = ((bf16[16,4,16,512]{3,2,1,0:T(8,128)(2,1)}), bf16[16,4,16,512]{3,2,1,0:T(8,128)(2,1)}, u32[]{:S(2)}, u32[]{:S(2)}) async-start(bf16[16,4,16,512]{3,2,1,0:T(8,128)(2,1)} %shared.1), calls=%async_computation.1 | async-start | bytes 2097152 | tf_op jit(solution)/shard_map/all_to_all | solution.py:222
  68.4 30.7 %collective-permute-start.2 = (bf16[128,1024]{1,0:T(8,128)(2,1)S(1)}, bf16[128,1024]{1,0:T(8,128)(2,1)S(1)}, u32[]{:S(2)}, u32[]{:S(2)}) collective-permute-start(bf16[128,1024]{1,0:T(8,128)(2,1)S(1)} %get-tuple-element.16), channel_id=1, source_target_pairs={{0,512},{64,576},{128,640},{192,704},{256,768},{320,832},{384,896}... | collective-permute-start | bytes 786440 | tf_op jit(solution)/shard_map/ppermute | solution.py:172
  80.3 18.8 %collective-permute-start.1 = (bf16[128,1024]{1,0:T(8,128)(2,1)S(1)}, bf16[128,1024]{1,0:T(8,128)(2,1)S(1)}, u32[]{:S(2)}, u32[]{:S(2)}) collective-permute-start(bf16[128,1024]{1,0:T(8,128)(2,1)S(1)} %get-tuple-element.17), channel_id=1, source_target_pairs={{0,512},{64,576},{128,640},{192,704},{256,768},{320,832},{384,896}... | collective-permute-start | bytes 786440 | tf_op jit(solution)/shard_map/ppermute | solution.py:172
  82.2 16.9 %collective-permute-start = (f32[2,8]{1,0:T(2,128)S(1)}, f32[2,8]{1,0:T(2,128)S(1)}, u32[]{:S(2)}, u32[]{:S(2)}) collective-permute-start(f32[2,8]{1,0:T(2,128)S(1)} %bitcast.43), channel_id=1, source_target_pairs={{0,512},{64,576},{128,640},{192,704},{256,768},{320,832},{384,896}... | collective-permute-start | bytes 200 | tf_op jit(solution)/shard_map/ppermute | solution.py:172
  90.1 10.1 %copy-start.7 = (bf16[1024,256]{1,0:T(8,128)(2,1)S(1)}, bf16[1024,256]{1,0:T(8,128)(2,1)}, u32[]{:S(2)}) copy-start(bf16[1024,256]{1,0:T(8,128)(2,1)} %get-tuple-element.8) | copy-start | bytes 1572868
  99.1 1.2 copy-start.4
  99.9 1.1 copy-start.6
  102.2 23.7 %collective-permute-start.6 = (bf16[256,512]{1,0:T(8,128)(2,1)}, bf16[256,512]{1,0:T(8,128)(2,1)}, u32[]{:S(2)}, u32[]{:S(2)}) collective-permute-start(bf16[256,512]{1,0:T(8,128)(2,1)} %convolution_convert_fusion.2), channel_id=1, source_target_pairs={{0,512},{64,576},{128,640},{192,704},{256,768},{320,832},{384,896}... | collective-permute-start | bytes 786440 | tf_op jit(solution)/shard_map/ppermute | solution.py:172
  113.6 1.4 copy-start.9
  116.7 19.5 %collective-permute-start.7 = (bf16[256,512]{1,0:T(8,128)(2,1)S(1)}, bf16[256,512]{1,0:T(8,128)(2,1)S(1)}, u32[]{:S(2)}, u32[]{:S(2)}) collective-permute-start(bf16[256,512]{1,0:T(8,128)(2,1)S(1)} %convolution_convert_fusion), channel_id=1, source_target_pairs={{0,512},{64,576},{128,640},{192,704},{256,768},{320,832},{384,896}... | collective-permute-start | bytes 786440 | tf_op jit(solution)/shard_map/ppermute | solution.py:172
  118.6 1.7 %copy-start.8 = (bf16[1024,256]{1,0:T(8,128)(2,1)S(1)}, bf16[1024,256]{1,0:T(8,128)(2,1)}, u32[]{:S(2)}) copy-start(bf16[1024,256]{1,0:T(8,128)(2,1)} %get-tuple-element.10) | copy-start | bytes 1572868

commit v6 on v4

--- a/solution.py
+++ b/solution.py
@@ -13,6 +13,8 @@
 VM = pl.BlockSpec(memory_space=pltpu.VMEM)
 SM = pl.BlockSpec(memory_space=pltpu.SMEM)
 
+PARAMS = pltpu.CompilerParams(vmem_limit_bytes=16 << 20)
+
 
 def cost(flops, nbytes):
     return pl.CostEstimate(flops=flops, bytes_accessed=nbytes, transcendentals=0)
@@ -34,6 +36,7 @@
         in_specs=[SM, VM],
         out_specs=VM,
         name="dequant",
+        compiler_params=PARAMS,
         cost_estimate=cost(weight.size, weight.size * 4),
     )(scales, weight)
 
@@ -156,6 +159,7 @@
         in_specs=[SM] + [VM] * len(blocks),
         out_specs=VM,
         name="shared",
+        compiler_params=PARAMS,
         cost_estimate=cost(2 * size * toks, size * 2),
     )(side, *blocks)
 
@@ -188,9 +192,10 @@
     routes, gates = routes[0, 0].T, gate_weights[0, 0].T
 
     packed = pack(routes, gates, grad)
-    blocks = [packed]
-    for k in range(1, RUN):
-        blocks.append(share(packed, k))
+    far = share(packed, 2)
+    near = share(packed, 1)
+    corner = share(far, 1)
+    blocks = [packed, near, far, corner]
     own_half = dequantize(down_weight[0, 0], block_scales[0, 0])
     other_half = partner(own_half)
 

time: 144 us -> 135 us (0.938)
  the two profiles are of different devices: /device:TPU:1 before, /device:TPU:128 now
where the time goes in v6:
time: 135 us
  waiting for transfers between devices  60.5 us (45%)
  starting transfers between devices  55.4 us (41%)
  Pallas kernels  6.92 us (5%)
  matrix products  6.33 us (5%)
  local copies, waits for them, and re-layouts  3.33 us (2%)
    ppermute x3, waiting for transfers between devices, partner(): return lax.ppermute(block, 'pipe', route)  37.9 us
    ppermute x3, waiting for transfers between devices, share(): return lax.ppermute(block, 'expert', [(i, i ^ 2 * k) for i in range(count)])  22.6 us
    ppermute x3, starting transfers between devices, partner(): return lax.ppermute(block, 'pipe', route)  21.1 us
    all_to_all x1, starting transfers between devices, on_device(): first = lax.all_to_all(first, 'expert', 0, 0, tiled=True).reshape(slots, -1)  15.5 us
    ppermute x3, starting transfers between devices, share(): return lax.ppermute(block, 'expert', [(i, i ^ 2 * k) for i in range(count)])  12.1 us
    all_to_all x1, starting transfers between devices, on_device(): lax.all_to_all(second, 'expert', 0, 0, tiled=True, axis_index_groups=groups)  6.71 us
  transfers between devices with their start and end apart: 8, of which 5 were waited for; matrix products, arithmetic and copies ran while one was open for 7% of the time, Pallas kernels for 3%

profile of v6, /device:TPU:128, one launch (start us, length us, event | category | flops | bytes accessed | tf_op | source)
XLA Modules:
  0.0 134.6 jit_solution(11360642304971285809)
XLA Ops:
  0.6 0.0 copy-start.3
  0.6 2.6 %direct.1 = bf16[64,16,512]{2,1,0:T(8,128)(2,1)} custom-call(s32[8,128]{1,0:T(8,128)} %bitcast.51, f32[8,128]{1,0:T(8,128)} %bitcast.53, bf16[128,1024]{1,0:T(8,128)(2,1)} %bitcast.49), custom_call_target="tpu_custom_call" | custom-call | flops 134217728 | bytes 1048576 | tf_op jit(solution)/shard_map/direct/pallas_call | solution.py:116
  3.2 15.5 %all-to-all-start = ((bf16[64,16,512]{2,1,0:T(8,128)(2,1)}), bf16[64,16,512]{2,1,0:T(8,128)(2,1)S(1)}, u32[]{:S(2)}, u32[]{:S(2)}) async-start(bf16[64,16,512]{2,1,0:T(8,128)(2,1)} %direct.1), calls=%async_computation | async-start | bytes 2097152 | tf_op jit(solution)/shard_map/all_to_all | solution.py:214
  18.7 1.6 %pack.1.refs_1_ = bf16[144,512]{1,0:T(8,128)(2,1)} custom-call(s32[8,128]{1,0:T(8,128)} %bitcast.52, f32[8,128]{1,0:T(8,128)} %bitcast.54, bf16[128,1024]{1,0:T(8,128)(2,1)} %bitcast.50), custom_call_target="tpu_custom_call" | custom-call | flops 65536 | bytes 262144 | tf_op jit(solution)/shard_map/pack/pallas_call | solution.py:68
  20.3 4.3 %collective-permute-start.2 = (bf16[144,512]{1,0:T(8,128)(2,1)}, bf16[144,512]{1,0:T(8,128)(2,1)S(1)}, u32[]{:S(2)}, u32[]{:S(2)}) collective-permute-start(bf16[144,512]{1,0:T(8,128)(2,1)} %pack.1.refs_1_), channel_id=1, source_target_pairs={{0,4},{1,5},{2,6},{3,7},{4,0},{5,1},{6,2},{7,3},{8,12},{9,13},{10,... | collective-permute-start | bytes 442376 | tf_op jit(solution)/shard_map/ppermute | solution.py:175
  24.6 2.5 %collective-permute-start.1 = (bf16[144,512]{1,0:T(8,128)(2,1)}, bf16[144,512]{1,0:T(8,128)(2,1)S(1)}, u32[]{:S(2)}, u32[]{:S(2)}) collective-permute-start(bf16[144,512]{1,0:T(8,128)(2,1)} %pack.1.refs_1_), channel_id=1, source_target_pairs={{0,2},{1,3},{2,0},{3,1},{4,6},{5,7},{6,4},{7,5},{8,10},{9,11},{10,... | collective-permute-start | bytes 442376 | tf_op jit(solution)/shard_map/ppermute | solution.py:175
  27.1 21.0 %collective-permute-done.2.refs_3_ = bf16[144,512]{1,0:T(8,128)(2,1)S(1)} collective-permute-done((bf16[144,512]{1,0:T(8,128)(2,1)}, bf16[144,512]{1,0:T(8,128)(2,1)S(1)}, u32[]{:S(2)}, u32[]{:S(2)}) %collective-permute-start.2) | collective-permute-done | bytes 147488 | tf_op jit(solution)/shard_map/ppermute | solution.py:175
  48.1 5.3 %collective-permute-start.3 = (bf16[144,512]{1,0:T(8,128)(2,1)S(1)}, bf16[144,512]{1,0:T(8,128)(2,1)S(1)}, u32[]{:S(2)}, u32[]{:S(2)}) collective-permute-start(bf16[144,512]{1,0:T(8,128)(2,1)S(1)} %collective-permute-done.2.refs_3_), channel_id=1, source_target_pairs={{0,2},{1,3},{2,0},{3,1},{4,6},{5,7},{6,4},{7,5},{8,10},{9,11},{10,... | collective-permute-start | bytes 442376 | tf_op jit(solution)/shard_map/ppermute | solution.py:175
  53.4 0.0 copy-done.3
  53.4 1.1 dynamic-slice_bitcast_fusion
  54.5 0.0 copy-start
  54.5 0.1 copy.9
  54.6 1.1 constant_dynamic-slice_fusion
  55.7 0.0 copy-start.1
  55.7 0.0 copy-start.2
  55.7 0.0 collective-permute-done.1.refs_2_
  55.7 1.6 %collective-permute-done.3.refs_4_ = bf16[144,512]{1,0:T(8,128)(2,1)S(1)} collective-permute-done((bf16[144,512]{1,0:T(8,128)(2,1)S(1)}, bf16[144,512]{1,0:T(8,128)(2,1)S(1)}, u32[]{:S(2)}, u32[]{:S(2)}) %collective-permute-start.3) | collective-permute-done | bytes 147488 | tf_op jit(solution)/shard_map/ppermute | solution.py:175
  57.3 0.0 copy-done
  57.3 1.9 %shared.1 = bf16[16,4,16,512]{3,2,1,0:T(8,128)(2,1)} custom-call(s32[1]{0:T(128)} %bitcast.8.refs_0_, bf16[144,512]{1,0:T(8,128)(2,1)S(1)} %copy-done, bf16[144,512]{1,0:T(8,128)(2,1)S(1)} %collective-permute-done.1.refs_2_, bf16[144,512]{1,0:T(8,128)(2,1)S(1)} %collective-permute-done.2.refs_3_, bf16[144,512]{1,0:T(8,128)(2,1)S(1)} %collective-permute-done.3.refs_4_), custom_call_target="tpu_custom_call" | custom-call | flops 134217728 | bytes 1048576 | tf_op jit(solution)/shard_map/shared/pallas_call | solution.py:156
  59.2 0.0 all-to-all-done
  59.2 0.0 copy-start.4
  59.2 1.0 copy-done.4
  60.2 6.7 %all-to-all-start.1 = ((bf16[16,4,16,512]{3,2,1,0:T(8,128)(2,1)}), bf16[16,4,16,512]{3,2,1,0:T(8,128)(2,1)S(1)}, u32[]{:S(2)}, u32[]{:S(2)}) async-start(bf16[16,4,16,512]{3,2,1,0:T(8,128)(2,1)} %shared.1), calls=%async_computation.1 | async-start | bytes 2097152 | tf_op jit(solution)/shard_map/all_to_all | solution.py:217
  66.9 0.0 copy-done.1
  67.0 0.0 copy-done.2
  67.0 0.8 dequant.1
  67.7 11.3 %collective-permute-start = (bf16[1024,256]{1,0:T(8,128)(2,1)S(1)}, bf16[1024,256]{1,0:T(8,128)(2,1)S(1)}, u32[]{:S(2)}, u32[]{:S(2)}) collective-permute-start(bf16[1024,256]{1,0:T(8,128)(2,1)S(1)} %dequant.1), channel_id=1, source_target_pairs={{0,512},{64,576},{128,640},{192,704},{256,768},{320,832},{384,896}... | collective-permute-start | bytes 1572872 | tf_op jit(solution)/shard_map/ppermute | solution.py:170
  79.0 0.0 copy-start.5
  79.0 23.8 %collective-permute-done = bf16[1024,256]{1,0:T(8,128)(2,1)S(1)} collective-permute-done((bf16[1024,256]{1,0:T(8,128)(2,1)S(1)}, bf16[1024,256]{1,0:T(8,128)(2,1)S(1)}, u32[]{:S(2)}, u32[]{:S(2)}) %collective-permute-start) | collective-permute-done | bytes 524320 | tf_op jit(solution)/shard_map/ppermute | solution.py:170
  102.8 0.2 maximum_select_fusion
  103.0 0.0 copy-done.5
  103.0 1.5 %convolution_convert_fusion.3 = bf16[256,512]{1,0:T(8,128)(2,1)S(1)} fusion(bf16[1024,256]{1,0:T(8,128)(2,1)} %get-tuple-element.8, bf16[1024,512]{1,0:T(8,128)(2,1)S(1)} %bitcast.46), kind=kOutput, calls=%fused_computation.5 | convolution fusion | flops 268566528 | bytes 1835008 | tf_op jit(solution)/shard_map/dot_general | solution.py:225
  104.5 0.0 copy-start.8
  104.5 1.6 %convolution_convert_fusion.2 = bf16[256,512]{1,0:T(8,128)(2,1)S(1)} fusion(bf16[1024,256]{1,0:T(8,128)(2,1)} %get-tuple-element.9, bf16[1024,512]{1,0:T(8,128)(2,1)S(1)} %bitcast.47), kind=kOutput, calls=%fused_computation.4 | convolution fusion | flops 268566528 | bytes 1835008 | tf_op jit(solution)/shard_map/dot_general | solution.py:223
  106.1 7.2 %collective-permute-start.4 = (bf16[256,512]{1,0:T(8,128)(2,1)S(1)}, bf16[256,512]{1,0:T(8,128)(2,1)S(1)}, u32[]{:S(2)}, u32[]{:S(2)}) collective-permute-start(bf16[256,512]{1,0:T(8,128)(2,1)S(1)} %convolution_convert_fusion.2), channel_id=1, source_target_pairs={{0,512},{64,576},{128,640},{192,704},{256,768},{320,832},{384,896}... | collective-permute-start | bytes 786440 | tf_op jit(solution)/shard_map/ppermute | solution.py:170
  113.3 0.0 all-to-all-done.1
  113.4 0.1 copy.10
  113.5 0.0 copy-done.8
  113.5 0.5 convolution_convert_fusion
  113.9 0.0 copy-start.6
  113.9 2.6 %collective-permute-start.5 = (bf16[256,512]{1,0:T(8,128)(2,1)S(1)}, bf16[256,512]{1,0:T(8,128)(2,1)S(1)}, u32[]{:S(2)}, u32[]{:S(2)}) collective-permute-start(bf16[256,512]{1,0:T(8,128)(2,1)S(1)} %convolution_convert_fusion), channel_id=1, source_target_pairs={{0,512},{64,576},{128,640},{192,704},{256,768},{320,832},{384,896}... | collective-permute-start | bytes 786440 | tf_op jit(solution)/shard_map/ppermute | solution.py:170
  116.6 0.7 fusion.1
  117.3 0.0 copy-done.6
  117.3 0.0 copy-start.7
  117.3 1.7 %fusion = bf16[1,1,1,1024,512]{4,3,2,1,0:T(8,128)(2,1)} fusion(f32[1024,512]{1,0:T(8,128)S(1)} %fusion.1, bf16[1024,512]{1,0:T(8,128)(2,1)S(1)} %bitcast.48, bf16[1024,512]{1,0:T(8,128)(2,1)S(1)} %maximum_select_fusion), kind=kOutput, calls=%fused_computation.1 | convolution fusion | flops 537919488 | bytes 4718592 | tf_op jit(solution)/shard_map/dot_general | solution.py:235
  119.0 0.0 copy-done.7
  119.0 0.5 convolution_convert_fusion.1
  119.4 9.3 %collective-permute-done.4 = bf16[256,512]{1,0:T(8,128)(2,1)S(1)} collective-permute-done((bf16[256,512]{1,0:T(8,128)(2,1)S(1)}, bf16[256,512]{1,0:T(8,128)(2,1)S(1)}, u32[]{:S(2)}, u32[]{:S(2)}) %collective-permute-start.4) | collective-permute-done | bytes 262176 | tf_op jit(solution)/shard_map/ppermute | solution.py:170
  128.8 0.1 add_convert_fusion.2
  128.8 4.8 %collective-permute-done.5 = bf16[256,512]{1,0:T(8,128)(2,1)S(1)} collective-permute-done((bf16[256,512]{1,0:T(8,128)(2,1)S(1)}, bf16[256,512]{1,0:T(8,128)(2,1)S(1)}, u32[]{:S(2)}, u32[]{:S(2)}) %collective-permute-start.5) | collective-permute-done | bytes 262176 | tf_op jit(solution)/shard_map/ppermute | solution.py:170
  133.6 0.1 add_convert_fusion.1
  133.7 0.9 maximum_bitcast_fusion
Async XLA Ops:
  0.6 52.8 %copy-start.3 = (bf16[1,1,1,1024,512]{4,3,2,1,0:T(8,128)(2,1)S(1)}, bf16[1,1,1,1024,512]{4,3,2,1,0:T(8,128)(2,1)}, u32[]{:S(2)}) copy-start(bf16[1,1,1,1024,512]{4,3,2,1,0:T(8,128)(2,1)} %param.9) | copy-start | bytes 3145732
  3.2 56.0 %all-to-all-start = ((bf16[64,16,512]{2,1,0:T(8,128)(2,1)}), bf16[64,16,512]{2,1,0:T(8,128)(2,1)S(1)}, u32[]{:S(2)}, u32[]{:S(2)}) async-start(bf16[64,16,512]{2,1,0:T(8,128)(2,1)} %direct.1), calls=%async_computation | async-start | bytes 2097152 | tf_op jit(solution)/shard_map/all_to_all | solution.py:214
  20.3 27.8 %collective-permute-start.2 = (bf16[144,512]{1,0:T(8,128)(2,1)}, bf16[144,512]{1,0:T(8,128)(2,1)S(1)}, u32[]{:S(2)}, u32[]{:S(2)}) collective-permute-start(bf16[144,512]{1,0:T(8,128)(2,1)} %pack.1.refs_1_), channel_id=1, source_target_pairs={{0,4},{1,5},{2,6},{3,7},{4,0},{5,1},{6,2},{7,3},{8,12},{9,13},{10,... | collective-permute-start | bytes 442376 | tf_op jit(solution)/shard_map/ppermute | solution.py:175
  24.6 31.0 %collective-permute-start.1 = (bf16[144,512]{1,0:T(8,128)(2,1)}, bf16[144,512]{1,0:T(8,128)(2,1)S(1)}, u32[]{:S(2)}, u32[]{:S(2)}) collective-permute-start(bf16[144,512]{1,0:T(8,128)(2,1)} %pack.1.refs_1_), channel_id=1, source_target_pairs={{0,2},{1,3},{2,0},{3,1},{4,6},{5,7},{6,4},{7,5},{8,10},{9,11},{10,... | collective-permute-start | bytes 442376 | tf_op jit(solution)/shard_map/ppermute | solution.py:175
  48.1 9.2 %collective-permute-start.3 = (bf16[144,512]{1,0:T(8,128)(2,1)S(1)}, bf16[144,512]{1,0:T(8,128)(2,1)S(1)}, u32[]{:S(2)}, u32[]{:S(2)}) collective-permute-start(bf16[144,512]{1,0:T(8,128)(2,1)S(1)} %collective-permute-done.2.refs_3_), channel_id=1, source_target_pairs={{0,2},{1,3},{2,0},{3,1},{4,6},{5,7},{6,4},{7,5},{8,10},{9,11},{10,... | collective-permute-start | bytes 442376 | tf_op jit(solution)/shard_map/ppermute | solution.py:175
  54.5 2.8 %copy-start = (bf16[144,512]{1,0:T(8,128)(2,1)S(1)}, bf16[144,512]{1,0:T(8,128)(2,1)}, u32[]{:S(2)}) copy-start(bf16[144,512]{1,0:T(8,128)(2,1)} %pack.1.refs_1_) | copy-start | bytes 442372
  55.7 11.3 %copy-start.1 = (bf16[1,1,256,1024]{3,2,1,0:T(8,128)(2,1)S(1)}, bf16[1,1,256,1024]{3,2,1,0:T(8,128)(2,1)}, u32[]{:S(2)}) copy-start(bf16[1,1,256,1024]{3,2,1,0:T(8,128)(2,1)} %param.10) | copy-start | bytes 1572868
  55.7 11.3 %copy-start.2 = (f32[1,1,2,8]{3,2,1,0:T(2,128)S(1)}, f32[1,1,2,8]{3,2,1,0:T(2,128)}, u32[]{:S(2)}) copy-start(f32[1,1,2,8]{3,2,1,0:T(2,128)} %param.11) | copy-start | bytes 196
  59.2 1.0 copy-start.4
  60.2 53.1 %all-to-all-start.1 = ((bf16[16,4,16,512]{3,2,1,0:T(8,128)(2,1)}), bf16[16,4,16,512]{3,2,1,0:T(8,128)(2,1)S(1)}, u32[]{:S(2)}, u32[]{:S(2)}) async-start(bf16[16,4,16,512]{3,2,1,0:T(8,128)(2,1)} %shared.1), calls=%async_computation.1 | async-start | bytes 2097152 | tf_op jit(solution)/shard_map/all_to_all | solution.py:217
  67.7 35.0 %collective-permute-start = (bf16[1024,256]{1,0:T(8,128)(2,1)S(1)}, bf16[1024,256]{1,0:T(8,128)(2,1)S(1)}, u32[]{:S(2)}, u32[]{:S(2)}) collective-permute-start(bf16[1024,256]{1,0:T(8,128)(2,1)S(1)} %dequant.1), channel_id=1, source_target_pairs={{0,512},{64,576},{128,640},{192,704},{256,768},{320,832},{384,896}... | collective-permute-start | bytes 1572872 | tf_op jit(solution)/shard_map/ppermute | solution.py:170
  79.0 24.0 %copy-start.5 = (bf16[64,16,512]{2,1,0:T(8,128)(2,1)S(1)}, bf16[64,16,512]{2,1,0:T(8,128)(2,1)}, u32[]{:S(2)}) copy-start(bf16[64,16,512]{2,1,0:T(8,128)(2,1)} %copy-done.4) | copy-start | bytes 3145732
  104.5 8.9 %copy-start.8 = (bf16[1024,256]{1,0:T(8,128)(2,1)S(1)}, bf16[1024,256]{1,0:T(8,128)(2,1)}, u32[]{:S(2)}) copy-start(bf16[1024,256]{1,0:T(8,128)(2,1)} %get-tuple-element.11) | copy-start | bytes 1572868
  106.1 22.7 %collective-permute-start.4 = (bf16[256,512]{1,0:T(8,128)(2,1)S(1)}, bf16[256,512]{1,0:T(8,128)(2,1)S(1)}, u32[]{:S(2)}, u32[]{:S(2)}) collective-permute-start(bf16[256,512]{1,0:T(8,128)(2,1)S(1)} %convolution_convert_fusion.2), channel_id=1, source_target_pairs={{0,512},{64,576},{128,640},{192,704},{256,768},{320,832},{384,896}... | collective-permute-start | bytes 786440 | tf_op jit(solution)/shard_map/ppermute | solution.py:170
  113.9 3.4 %copy-start.6 = (bf16[64,16,512]{2,1,0:T(8,128)(2,1)S(1)}, bf16[64,16,512]{2,1,0:T(8,128)(2,1)}, u32[]{:S(2)}) copy-start(bf16[64,16,512]{2,1,0:T(8,128)(2,1)} %copy-done.4) | copy-start | bytes 3145732
  113.9 19.7 %collective-permute-start.5 = (bf16[256,512]{1,0:T(8,128)(2,1)S(1)}, bf16[256,512]{1,0:T(8,128)(2,1)S(1)}, u32[]{:S(2)}, u32[]{:S(2)}) collective-permute-start(bf16[256,512]{1,0:T(8,128)(2,1)S(1)} %convolution_convert_fusion), channel_id=1, source_target_pairs={{0,512},{64,576},{128,640},{192,704},{256,768},{320,832},{384,896}... | collective-permute-start | bytes 786440 | tf_op jit(solution)/shard_map/ppermute | solution.py:170
  117.3 1.7 %copy-start.7 = (bf16[1024,256]{1,0:T(8,128)(2,1)S(1)}, bf16[1024,256]{1,0:T(8,128)(2,1)}, u32[]{:S(2)}) copy-start(bf16[1024,256]{1,0:T(8,128)(2,1)} %get-tuple-element.10) | copy-start | bytes 1572868

commit v7 on v6

--- a/solution.py
+++ b/solution.py
@@ -207,23 +207,31 @@
         send = lax.dynamic_slice_in_dim(x, (1 - upper) * (ff // 2), ff // 2, 1)
         return keep, send
 
-    turned = act.reshape(-1, RUN, 2, cap, ff).transpose(0, 2, 1, 3, 4).reshape(slots, ff)
-    pieces = [halves(act), halves(turned)]
+    near_half = lax.optimization_barrier(halves(act))
 
     first = dispatch_direct(routes, gates, grad, experts, cap)
     first = lax.all_to_all(first, "expert", 0, 0, tiled=True).reshape(slots, -1)
-    pieces, blocks[0] = lax.optimization_barrier((pieces, blocks[0]))
+    near_half, blocks[0] = lax.optimization_barrier((near_half, blocks[0]))
     second = dispatch_shared(side, blocks, toks, experts, cap)
     second = lax.all_to_all(
         second, "expert", 0, 0, tiled=True, axis_index_groups=groups
     ).reshape(slots, -1)
 
     sent, kept = [], []
-    for (keep, send), rows in zip(pieces, (first, second)):
+    keep, send = near_half
+    for c, rows in enumerate((first, second)):
         part = lax.dot_general(send, rows, ROWS_ROWS, preferred_element_type=F32).astype(BF)
         sent.append(partner(part))
         part = lax.dot_general(keep, rows, ROWS_ROWS, preferred_element_type=F32)
         kept.append(lax.optimization_barrier(part.astype(BF)))
+        if c == 0:
+            keep, send, _ = lax.optimization_barrier((keep, send, kept[0]))
+            keep, send = (
+                x.reshape(-1, RUN, 2, cap, ff // 2)
+                .transpose(0, 2, 1, 3, 4)
+                .reshape(slots, ff // 2)
+                for x in (keep, send)
+            )
     whole = jnp.where(
         upper == 1,
         jnp.concatenate([other_half, own_half], axis=1),

time: 135 us -> 138 us (1.022)
  the two profiles are of different devices: /device:TPU:128 before, /device:TPU:132 now
where the time goes in v7:
time: 138 us; the launch traced here: 137 us
  waiting for transfers between devices  61.1 us (44%)
  starting transfers between devices  55.2 us (40%)
  Pallas kernels  6.91 us (5%)
  matrix products  5.96 us (4%)
  other arithmetic  3.39 us (2%)
  local copies, waits for them, and re-layouts  3.38 us (2%)
    ppermute x3, waiting for transfers between devices, partner(): return lax.ppermute(block, 'pipe', route)  37.2 us
    ppermute x3, waiting for transfers between devices, share(): return lax.ppermute(block, 'expert', [(i, i ^ 2 * k) for i in range(count)])  23.9 us
    ppermute x3, starting transfers between devices, partner(): return lax.ppermute(block, 'pipe', route)  21.6 us
    all_to_all x1, starting transfers between devices, on_device(): first = lax.all_to_all(first, 'expert', 0, 0, tiled=True).reshape(slots, -1)  15 us
    ppermute x3, starting transfers between devices, share(): return lax.ppermute(block, 'expert', [(i, i ^ 2 * k) for i in range(count)])  12.2 us
    all_to_all x1, starting transfers between devices, on_device(): lax.all_to_all(second, 'expert', 0, 0, tiled=True, axis_index_groups=groups)  6.43 us
  transfers between devices with their start and end apart: 8, of which 5 were waited for; matrix products, arithmetic and copies ran while one was open for 8% of the time, Pallas kernels for 3%

profile of v7, /device:TPU:132, one launch (start us, length us, event | category | flops | bytes accessed | tf_op | source)
XLA Modules:
  0.0 136.9 jit_solution(13563841785881346589)
XLA Ops:
  0.6 0.0 copy-start.7
  0.6 2.6 %direct.1 = bf16[64,16,512]{2,1,0:T(8,128)(2,1)} custom-call(s32[8,128]{1,0:T(8,128)} %bitcast.57, f32[8,128]{1,0:T(8,128)} %bitcast.59, bf16[128,1024]{1,0:T(8,128)(2,1)} %bitcast.53), custom_call_target="tpu_custom_call" | custom-call | flops 134217728 | bytes 1048576 | tf_op jit(solution)/shard_map/direct/pallas_call | solution.py:116
  3.2 15.0 %all-to-all-start = ((bf16[64,16,512]{2,1,0:T(8,128)(2,1)}), bf16[64,16,512]{2,1,0:T(8,128)(2,1)S(1)}, u32[]{:S(2)}, u32[]{:S(2)}) async-start(bf16[64,16,512]{2,1,0:T(8,128)(2,1)} %direct.1), calls=%async_computation | async-start | bytes 2097152 | tf_op jit(solution)/shard_map/all_to_all | solution.py:213
  18.2 1.6 %pack.1.refs_1_ = bf16[144,512]{1,0:T(8,128)(2,1)} custom-call(s32[8,128]{1,0:T(8,128)} %bitcast.58, f32[8,128]{1,0:T(8,128)} %bitcast.60, bf16[128,1024]{1,0:T(8,128)(2,1)} %bitcast.54), custom_call_target="tpu_custom_call" | custom-call | flops 65536 | bytes 262144 | tf_op jit(solution)/shard_map/pack/pallas_call | solution.py:68
  19.9 0.0 copy-start
  19.9 4.4 %collective-permute-start.2 = (bf16[144,512]{1,0:T(8,128)(2,1)}, bf16[144,512]{1,0:T(8,128)(2,1)S(1)}, u32[]{:S(2)}, u32[]{:S(2)}) collective-permute-start(bf16[144,512]{1,0:T(8,128)(2,1)} %pack.1.refs_1_), channel_id=1, source_target_pairs={{0,4},{1,5},{2,6},{3,7},{4,0},{5,1},{6,2},{7,3},{8,12},{9,13},{10,... | collective-permute-start | bytes 442376 | tf_op jit(solution)/shard_map/ppermute | solution.py:175
  24.3 2.5 %collective-permute-start.1 = (bf16[144,512]{1,0:T(8,128)(2,1)}, bf16[144,512]{1,0:T(8,128)(2,1)S(1)}, u32[]{:S(2)}, u32[]{:S(2)}) collective-permute-start(bf16[144,512]{1,0:T(8,128)(2,1)} %pack.1.refs_1_), channel_id=1, source_target_pairs={{0,2},{1,3},{2,0},{3,1},{4,6},{5,7},{6,4},{7,5},{8,10},{9,11},{10,... | collective-permute-start | bytes 442376 | tf_op jit(solution)/shard_map/ppermute | solution.py:175
  26.7 20.9 %collective-permute-done.2.refs_3_ = bf16[144,512]{1,0:T(8,128)(2,1)S(1)} collective-permute-done((bf16[144,512]{1,0:T(8,128)(2,1)}, bf16[144,512]{1,0:T(8,128)(2,1)S(1)}, u32[]{:S(2)}, u32[]{:S(2)}) %collective-permute-start.2) | collective-permute-done | bytes 147488 | tf_op jit(solution)/shard_map/ppermute | solution.py:175
  47.6 5.3 %collective-permute-start.3 = (bf16[144,512]{1,0:T(8,128)(2,1)S(1)}, bf16[144,512]{1,0:T(8,128)(2,1)S(1)}, u32[]{:S(2)}, u32[]{:S(2)}) collective-permute-start(bf16[144,512]{1,0:T(8,128)(2,1)S(1)} %collective-permute-done.2.refs_3_), channel_id=1, source_target_pairs={{0,2},{1,3},{2,0},{3,1},{4,6},{5,7},{6,4},{7,5},{8,10},{9,11},{10,... | collective-permute-start | bytes 442376 | tf_op jit(solution)/shard_map/ppermute | solution.py:175
  53.0 0.0 copy-done.7
  53.0 0.9 dynamic-slice_bitcast_fusion
  53.9 0.0 copy-start.1
  53.9 0.0 copy-start.2
  53.9 0.0 collective-permute-done.1.refs_2_
  53.9 3.1 %collective-permute-done.3.refs_4_ = bf16[144,512]{1,0:T(8,128)(2,1)S(1)} collective-permute-done((bf16[144,512]{1,0:T(8,128)(2,1)S(1)}, bf16[144,512]{1,0:T(8,128)(2,1)S(1)}, u32[]{:S(2)}, u32[]{:S(2)}) %collective-permute-start.3) | collective-permute-done | bytes 147488 | tf_op jit(solution)/shard_map/ppermute | solution.py:175
  56.9 0.0 copy-done
  56.9 1.9 %shared.1 = bf16[16,4,16,512]{3,2,1,0:T(8,128)(2,1)} custom-call(s32[1]{0:T(128)} %bitcast.8.refs_0_, bf16[144,512]{1,0:T(8,128)(2,1)S(1)} %copy-done, bf16[144,512]{1,0:T(8,128)(2,1)S(1)} %collective-permute-done.1.refs_2_, bf16[144,512]{1,0:T(8,128)(2,1)S(1)} %collective-permute-done.2.refs_3_, bf16[144,512]{1,0:T(8,128)(2,1)S(1)} %collective-permute-done.3.refs_4_), custom_call_target="tpu_custom_call" | custom-call | flops 134217728 | bytes 1048576 | tf_op jit(solution)/shard_map/shared/pallas_call | solution.py:156
  58.9 0.0 all-to-all-done
  58.9 0.0 copy-start.3
  58.9 1.0 copy-done.3
  59.9 6.4 %all-to-all-start.1 = ((bf16[16,4,16,512]{3,2,1,0:T(8,128)(2,1)}), bf16[16,4,16,512]{3,2,1,0:T(8,128)(2,1)S(1)}, u32[]{:S(2)}, u32[]{:S(2)}) async-start(bf16[16,4,16,512]{3,2,1,0:T(8,128)(2,1)} %shared.1), calls=%async_computation.1 | async-start | bytes 2097152 | tf_op jit(solution)/shard_map/all_to_all | solution.py:216
  66.3 0.0 copy-done.1
  66.3 0.0 copy-done.2
  66.3 0.8 dequant.1
  67.1 11.9 %collective-permute-start = (bf16[1024,256]{1,0:T(8,128)(2,1)S(1)}, bf16[1024,256]{1,0:T(8,128)(2,1)}, u32[]{:S(2)}, u32[]{:S(2)}) collective-permute-start(bf16[1024,256]{1,0:T(8,128)(2,1)S(1)} %dequant.1), channel_id=1, source_target_pairs={{0,512},{64,576},{128,640},{192,704},{256,768},{320,832},{384,896}... | collective-permute-start | bytes 1572872 | tf_op jit(solution)/shard_map/ppermute | solution.py:170
  79.0 0.0 copy-start.4
  79.0 0.0 copy-start.6
  79.0 23.8 %collective-permute-done = bf16[1024,256]{1,0:T(8,128)(2,1)} collective-permute-done((bf16[1024,256]{1,0:T(8,128)(2,1)S(1)}, bf16[1024,256]{1,0:T(8,128)(2,1)}, u32[]{:S(2)}, u32[]{:S(2)}) %collective-permute-start) | collective-permute-done | bytes 524320 | tf_op jit(solution)/shard_map/ppermute | solution.py:170
  102.8 1.4 %maximum_select_fusion = bf16[1024,512]{1,0:T(8,128)(2,1)S(1)} fusion(bf16[1024,256]{1,0:T(8,128)(2,1)S(1)} %dequant.1, bf16[1024,256]{1,0:T(8,128)(2,1)} %collective-permute-done, pred[]{:T(512)S(6)} %eq.5), kind=kLoop, calls=%fused_computation.6 | loop fusion | flops 4718592 | bytes 2097153 | tf_op jit(solution)/shard_map/jit(_where)/select_n | solution.py:235
  104.3 0.0 copy-done.4
  104.3 1.5 %convolution_convert_fusion.3 = bf16[256,512]{1,0:T(8,128)(2,1)S(1)} fusion(bf16[1024,256]{1,0:T(8,128)(2,1)} %get-tuple-element.14, bf16[1024,512]{1,0:T(8,128)(2,1)S(1)} %bitcast.48), kind=kOutput, calls=%fused_computation.5 | convolution fusion | flops 268566528 | bytes 1835008 | tf_op jit(solution)/shard_map/dot_general | solution.py:225
  105.8 0.1 copy.11
  105.9 0.0 copy-done.6
  105.9 0.9 copy.10
  106.7 1.2 convolution_convert_fusion.2
  107.9 7.2 %collective-permute-start.4 = (bf16[256,512]{1,0:T(8,128)(2,1)}, bf16[256,512]{1,0:T(8,128)(2,1)}, u32[]{:S(2)}, u32[]{:S(2)}) collective-permute-start(bf16[256,512]{1,0:T(8,128)(2,1)} %convolution_convert_fusion.2), channel_id=1, source_target_pairs={{0,512},{64,576},{128,640},{192,704},{256,768},{320,832},{384,896}... | collective-permute-start | bytes 786440 | tf_op jit(solution)/shard_map/ppermute | solution.py:170
  115.1 0.0 all-to-all-done.1
  115.2 0.5 convolution_convert_fusion
  115.6 2.5 %collective-permute-start.5 = (bf16[256,512]{1,0:T(8,128)(2,1)S(1)}, bf16[256,512]{1,0:T(8,128)(2,1)S(1)}, u32[]{:S(2)}, u32[]{:S(2)}) collective-permute-start(bf16[256,512]{1,0:T(8,128)(2,1)S(1)} %convolution_convert_fusion), channel_id=1, source_target_pairs={{0,512},{64,576},{128,640},{192,704},{256,768},{320,832},{384,896}... | collective-permute-start | bytes 786440 | tf_op jit(solution)/shard_map/ppermute | solution.py:170
  118.1 0.1 copy.9
  118.2 0.0 copy-start.5
  118.2 0.7 fusion.1
  118.9 0.5 copy-done.5
  119.5 0.0 copy-start.8
  119.5 1.7 %fusion = bf16[1,1,1,1024,512]{4,3,2,1,0:T(8,128)(2,1)} fusion(f32[1024,512]{1,0:T(8,128)S(1)} %fusion.1, bf16[1024,512]{1,0:T(8,128)(2,1)S(1)} %bitcast.50, bf16[1024,512]{1,0:T(8,128)(2,1)S(1)} %maximum_select_fusion), kind=kOutput, calls=%fused_computation.1 | convolution fusion | flops 537919488 | bytes 4718592 | tf_op jit(solution)/shard_map/dot_general | solution.py:243
  121.1 0.0 copy-done.8
  121.1 0.5 convolution_convert_fusion.1
  121.6 9.6 %collective-permute-done.4 = bf16[256,512]{1,0:T(8,128)(2,1)} collective-permute-done((bf16[256,512]{1,0:T(8,128)(2,1)}, bf16[256,512]{1,0:T(8,128)(2,1)}, u32[]{:S(2)}, u32[]{:S(2)}) %collective-permute-start.4) | collective-permute-done | bytes 262176 | tf_op jit(solution)/shard_map/ppermute | solution.py:170
  131.2 1.0 add_convert_fusion.2
  132.2 3.7 %collective-permute-done.5 = bf16[256,512]{1,0:T(8,128)(2,1)S(1)} collective-permute-done((bf16[256,512]{1,0:T(8,128)(2,1)S(1)}, bf16[256,512]{1,0:T(8,128)(2,1)S(1)}, u32[]{:S(2)}, u32[]{:S(2)}) %collective-permute-start.5) | collective-permute-done | bytes 262176 | tf_op jit(solution)/shard_map/ppermute | solution.py:170
  135.9 0.1 add_convert_fusion.1
  136.0 0.9 maximum_bitcast_fusion
Async XLA Ops:
  0.6 52.4 %copy-start.7 = (bf16[1,1,1,1024,512]{4,3,2,1,0:T(8,128)(2,1)S(1)}, bf16[1,1,1,1024,512]{4,3,2,1,0:T(8,128)(2,1)}, u32[]{:S(2)}) copy-start(bf16[1,1,1,1024,512]{4,3,2,1,0:T(8,128)(2,1)} %param.9) | copy-start | bytes 3145732
  3.2 55.6 %all-to-all-start = ((bf16[64,16,512]{2,1,0:T(8,128)(2,1)}), bf16[64,16,512]{2,1,0:T(8,128)(2,1)S(1)}, u32[]{:S(2)}, u32[]{:S(2)}) async-start(bf16[64,16,512]{2,1,0:T(8,128)(2,1)} %direct.1), calls=%async_computation | async-start | bytes 2097152 | tf_op jit(solution)/shard_map/all_to_all | solution.py:213
  19.9 37.1 %copy-start = (bf16[144,512]{1,0:T(8,128)(2,1)S(1)}, bf16[144,512]{1,0:T(8,128)(2,1)}, u32[]{:S(2)}) copy-start(bf16[144,512]{1,0:T(8,128)(2,1)} %pack.1.refs_1_) | copy-start | bytes 442372
  19.9 27.8 %collective-permute-start.2 = (bf16[144,512]{1,0:T(8,128)(2,1)}, bf16[144,512]{1,0:T(8,128)(2,1)S(1)}, u32[]{:S(2)}, u32[]{:S(2)}) collective-permute-start(bf16[144,512]{1,0:T(8,128)(2,1)} %pack.1.refs_1_), channel_id=1, source_target_pairs={{0,4},{1,5},{2,6},{3,7},{4,0},{5,1},{6,2},{7,3},{8,12},{9,13},{10,... | collective-permute-start | bytes 442376 | tf_op jit(solution)/shard_map/ppermute | solution.py:175
  24.3 29.6 %collective-permute-start.1 = (bf16[144,512]{1,0:T(8,128)(2,1)}, bf16[144,512]{1,0:T(8,128)(2,1)S(1)}, u32[]{:S(2)}, u32[]{:S(2)}) collective-permute-start(bf16[144,512]{1,0:T(8,128)(2,1)} %pack.1.refs_1_), channel_id=1, source_target_pairs={{0,2},{1,3},{2,0},{3,1},{4,6},{5,7},{6,4},{7,5},{8,10},{9,11},{10,... | collective-permute-start | bytes 442376 | tf_op jit(solution)/shard_map/ppermute | solution.py:175
  47.6 9.3 %collective-permute-start.3 = (bf16[144,512]{1,0:T(8,128)(2,1)S(1)}, bf16[144,512]{1,0:T(8,128)(2,1)S(1)}, u32[]{:S(2)}, u32[]{:S(2)}) collective-permute-start(bf16[144,512]{1,0:T(8,128)(2,1)S(1)} %collective-permute-done.2.refs_3_), channel_id=1, source_target_pairs={{0,2},{1,3},{2,0},{3,1},{4,6},{5,7},{6,4},{7,5},{8,10},{9,11},{10,... | collective-permute-start | bytes 442376 | tf_op jit(solution)/shard_map/ppermute | solution.py:175
  53.9 12.4 %copy-start.1 = (bf16[1,1,256,1024]{3,2,1,0:T(8,128)(2,1)S(1)}, bf16[1,1,256,1024]{3,2,1,0:T(8,128)(2,1)}, u32[]{:S(2)}) copy-start(bf16[1,1,256,1024]{3,2,1,0:T(8,128)(2,1)} %param.10) | copy-start | bytes 1572868
  53.9 12.4 %copy-start.2 = (f32[1,1,2,8]{3,2,1,0:T(2,128)S(1)}, f32[1,1,2,8]{3,2,1,0:T(2,128)}, u32[]{:S(2)}) copy-start(f32[1,1,2,8]{3,2,1,0:T(2,128)} %param.11) | copy-start | bytes 196
  58.9 1.0 copy-start.3
  59.9 55.3 %all-to-all-start.1 = ((bf16[16,4,16,512]{3,2,1,0:T(8,128)(2,1)}), bf16[16,4,16,512]{3,2,1,0:T(8,128)(2,1)S(1)}, u32[]{:S(2)}, u32[]{:S(2)}) async-start(bf16[16,4,16,512]{3,2,1,0:T(8,128)(2,1)} %shared.1), calls=%async_computation.1 | async-start | bytes 2097152 | tf_op jit(solution)/shard_map/all_to_all | solution.py:216
  67.1 35.8 %collective-permute-start = (bf16[1024,256]{1,0:T(8,128)(2,1)S(1)}, bf16[1024,256]{1,0:T(8,128)(2,1)}, u32[]{:S(2)}, u32[]{:S(2)}) collective-permute-start(bf16[1024,256]{1,0:T(8,128)(2,1)S(1)} %dequant.1), channel_id=1, source_target_pairs={{0,512},{64,576},{128,640},{192,704},{256,768},{320,832},{384,896}... | collective-permute-start | bytes 1572872 | tf_op jit(solution)/shard_map/ppermute | solution.py:170
  79.0 25.3 %copy-start.4 = (bf16[64,16,512]{2,1,0:T(8,128)(2,1)S(1)}, bf16[64,16,512]{2,1,0:T(8,128)(2,1)}, u32[]{:S(2)}) copy-start(bf16[64,16,512]{2,1,0:T(8,128)(2,1)} %copy-done.3) | copy-start | bytes 3145732
  79.0 26.9 %copy-start.6 = (bf16[1024,256]{1,0:T(8,128)(2,1)S(1)}, bf16[1024,256]{1,0:T(8,128)(2,1)}, u32[]{:S(2)}) copy-start(bf16[1024,256]{1,0:T(8,128)(2,1)} %get-tuple-element.14) | copy-start | bytes 1572868
  107.9 23.3 %collective-permute-start.4 = (bf16[256,512]{1,0:T(8,128)(2,1)}, bf16[256,512]{1,0:T(8,128)(2,1)}, u32[]{:S(2)}, u32[]{:S(2)}) collective-permute-start(bf16[256,512]{1,0:T(8,128)(2,1)} %convolution_convert_fusion.2), channel_id=1, source_target_pairs={{0,512},{64,576},{128,640},{192,704},{256,768},{320,832},{384,896}... | collective-permute-start | bytes 786440 | tf_op jit(solution)/shard_map/ppermute | solution.py:170
  115.6 20.3 %collective-permute-start.5 = (bf16[256,512]{1,0:T(8,128)(2,1)S(1)}, bf16[256,512]{1,0:T(8,128)(2,1)S(1)}, u32[]{:S(2)}, u32[]{:S(2)}) collective-permute-start(bf16[256,512]{1,0:T(8,128)(2,1)S(1)} %convolution_convert_fusion), channel_id=1, source_target_pairs={{0,512},{64,576},{128,640},{192,704},{256,768},{320,832},{384,896}... | collective-permute-start | bytes 786440 | tf_op jit(solution)/shard_map/ppermute | solution.py:170
  118.2 1.2 copy-start.5
  119.5 1.7 %copy-start.8 = (bf16[8,2,4,16,256]{4,3,2,1,0:T(8,128)(2,1)S(1)}, bf16[8,2,4,16,256]{4,3,2,1,0:T(8,128)(2,1)}, u32[]{:S(2)}) copy-start(bf16[8,2,4,16,256]{4,3,2,1,0:T(8,128)(2,1)} %copy.10) | copy-start | bytes 1572868
